TPU v7x, 32 devices: a whole 2x2x4 slice. The times are simulated.
32 devices in a mesh: group: 16 (over z, y, core), tp: 2 (over x).
Axes of the slice: x: 2, y: 2, z: 4, core: 2. Of those that a mesh axis runs over, the one named last changes fastest.
Arguments:
- tokens: bfloat16 [8192, 3200], P('group', 'tp'), may hold values from -6 to 6
- norm_gain: bfloat16 [3200], P('tp'), may hold values from 0.25 to 1.75
- w_qkv: bfloat16 [3200, 3, 2048], P('group', None, 'tp'), may hold values from -1 to 1, as said below
- qk_gain: float32 [2, 2048], P(None, 'tp'), may hold values from 0.5 to 8
- w_out: bfloat16 [2048, 3200], P('tp', 'group'), may hold values from -0.125 to 0.125
- layer_scale: float32 [3200], P('tp'), may hold values from 0.3 to 1.5
- request: int32 [8192], P('group'), may hold values from 0 to 8191, as said below
- owner: int32 [8192, 1], P('group'), may hold values from 0 to 15; in each aligned block of 512 rows (0 to 511, 512 to 1023, ...) at most 64 rows name the same one
Outputs:
- routed: bfloat16 [16, 16, 64, 3200], P('group', None, None, 'tp')
Inputs may be any that keep to these rules, and one draw needn't show every extreme that they name: Requests never cross a block of 1024 rows starting at a multiple of 1024, and blocks share none; in each such block exactly one request holds rows on both sides of its middle, at most 128 on each side, exactly 128 on each side in the first block; the first row's number is 0 and the last row's is 8191. Among one group's 512 rows at most 64 name the same owner; some owner is named by exactly 64 rows of some group. `w_qkv`: column scales of the projections vary across the columns.
All inputs are finite; a program needn't handle non-finite values.
Results may differ from a plain program's by a relative error of at most 0.0117.
The roundings to bfloat16 on the way count: a program that leaves them out, or rounds other values in their place, can miss the bound.
Values may be sent and summed in bfloat16 or wider, within the bound.
A program may use at most 128 MiB of HBM per device.

v0:
```python
import math

import jax
import jax.numpy as jnp
from jax import lax
from jax.sharding import PartitionSpec as P

HD = 128
SHARE = 128


def swapped(value, axis, apart):
    mask = 2**apart
    pairs = [(source, source ^ mask) for source in range(lax.axis_size(axis))]
    return lax.ppermute(value, axis, pairs)


def shards(tokens, norm_gain, w_qkv, qk_gain, w_out, layer_scale, request, owner):
    rows = tokens.shape[0]
    feat_local = tokens.shape[1]
    tp_count = lax.axis_size("tp")
    group_count = lax.axis_size("group")
    local_width = w_qkv.shape[2]
    head_count = local_width // HD
    whole, gain_all = (
        lax.all_gather(tokens, "tp", axis=1, tiled=True),
        lax.all_gather(norm_gain.reshape(1, feat_local), "tp", axis=1, tiled=True),
    )
    xwide = whole.astype(jnp.float32)
    stat = jnp.mean(xwide * xwide, axis=-1, keepdims=True)
    normed = (xwide * lax.rsqrt(stat + 1e-06) * gain_all.astype(jnp.float32)).astype(jnp.bfloat16)
    piece = lax.all_gather(w_qkv, "group", axis=0, tiled=True)
    qkv = jnp.dot(
        normed, piece.reshape(piece.shape[0], 3 * local_width), preferred_element_type=jnp.float32
    ).reshape(rows, 3, local_width)
    query = qkv[:, 0, :]
    key_rows = qkv[:, 1, :]
    value = qkv[:, 2, :].astype(jnp.bfloat16)
    qsum, ksum = lax.psum(
        (jnp.sum(query * query, axis=-1), jnp.sum(key_rows * key_rows, axis=-1)), "tp"
    )
    total_width = local_width * tp_count
    qnorm = (query * lax.rsqrt(qsum / total_width + 1e-06)[:, None] * qk_gain[0]).astype(
        jnp.bfloat16
    )
    knorm = (key_rows * lax.rsqrt(ksum / total_width + 1e-06)[:, None] * qk_gain[1]).astype(
        jnp.bfloat16
    )
    parity = lax.axis_index("group") % 2
    seam = jnp.where(parity == 0, rows - SHARE, 0).astype(jnp.int32)
    key_window = lax.dynamic_slice_in_dim(knorm, seam, SHARE, 0)
    value_window = lax.dynamic_slice_in_dim(value, seam, SHARE, 0)
    id_window = lax.dynamic_slice_in_dim(request, seam, SHARE, 0)
    paired, paired_ids = swapped((jnp.stack([key_window, value_window]), id_window), "group", 0)
    all_keys = jnp.concatenate([knorm, paired[0]], axis=0)
    all_values = jnp.concatenate([value, paired[1]], axis=0)
    all_ids = jnp.concatenate([request, paired_ids], axis=0)
    qheads = qnorm.reshape(rows, head_count, HD)
    kheads = all_keys.reshape(rows + SHARE, head_count, HD)
    vheads = all_values.reshape(rows + SHARE, head_count, HD)
    scores = jnp.einsum(
        "qhd,khd->hqk", qheads, kheads, preferred_element_type=jnp.float32
    ) / math.sqrt(HD)
    same = request[:, None] == all_ids[None, :]
    scores = jnp.where(same[None], scores, -jnp.inf)
    top = jnp.max(scores, axis=-1, keepdims=True)
    expo = jnp.exp(scores - top)
    probs = (expo / jnp.sum(expo, axis=-1, keepdims=True)).astype(jnp.bfloat16)
    attended = jnp.einsum("hqk,khd->qhd", probs, vheads, preferred_element_type=jnp.float32)
    attended = attended.astype(jnp.bfloat16).reshape(rows, local_width)
    partial_terms = jnp.dot(
        attended,
        lax.all_gather(w_out, "group", axis=1, tiled=True),
        preferred_element_type=jnp.float32,
    )
    mine = lax.psum_scatter(
        partial_terms.astype(jnp.bfloat16), "tp", scatter_dimension=1, tiled=True
    ).astype(jnp.float32)
    mixed = (tokens.astype(jnp.float32) + layer_scale * mine).astype(jnp.bfloat16)
    capacity = max(2, 2 * rows // group_count)
    target = owner[:, 0]
    onehot = (target[:, None] == jnp.arange(group_count, dtype=jnp.int32)[None, :]).astype(
        jnp.int32
    )
    slot = jnp.sum((jnp.cumsum(onehot, axis=0) - onehot) * onehot, axis=-1)
    outbox = (
        jnp.zeros((group_count, capacity, feat_local), jnp.bfloat16).at[target, slot].set(mixed)
    )
    inbox = lax.all_to_all(outbox, "group", split_axis=0, concat_axis=0, tiled=True)
    return inbox[None]


def solution(mesh):
    in_specs = (
        P("group", "tp"),
        P("tp"),
        P("group", None, "tp"),
        P(None, "tp"),
        P("tp", "group"),
        P("tp"),
        P("group"),
        P("group", None),
    )
    out_specs = P("group", None, None, "tp")
    return jax.shard_map(shards, mesh=mesh, in_specs=in_specs, out_specs=out_specs, check_vma=False)
```

profile of v0, /device:TPU:1, one launch (start us, length us, event | category | flops | bytes accessed | tf_op | source)
XLA Modules:
  0.0 463.1 jit_solution(18097618292027908334)
XLA Ops:
  6.6 0.7 all-gather.5.cloned.1.call-update
  7.3 0.7 all-gather.7.cloned.1.call-update
  8.1 0.7 all-gather.9.cloned.1.call-update
  10.5 5.0 %all-reduce = bf16[3200]{0:T(1024)(128)(2,1)S(1)} all-reduce(bf16[3200]{0:T(1024)(128)(2,1)S(1)} %dynamic-update-slice), channel_id=2, replica_groups=mesh['group'=16,'tp'=2] {'tp'}, use_global_device_ids=true, to_apply=%add | all-reduce | flops 3200 | bytes 12800
  15.6 1.0 broadcast_compare_fusion
  16.6 40.9 %all-gather.5.cloned.1.call-done = bf16[512,3200]{0,1:T(8,128)(2,1)} async-done(((bf16[512,1600]{0,1:T(8,128)(2,1)}), bf16[512,3200]{0,1:T(8,128)(2,1)}) %all-gather.5.cloned.1.call-update) | async-done | bytes 3276816 | tf_op jit(solution)/shard_map/all_gather | solution.py:26
  57.4 2.7 fusion.4
  60.1 101.9 %all-gather.7.cloned.1.call-done = bf16[3200,3,1024]{2,0,1:T(8,128)(2,1)} async-done(((bf16[200,3,1024]{2,0,1:T(8,128)(2,1)}), bf16[3200,3,1024]{2,0,1:T(8,128)(2,1)}) %all-gather.7.cloned.1.call-update) | async-done | bytes 19660816 | tf_op jit(solution)/shard_map/all_gather | solution.py:32
  162.1 24.0 %copy.25 = bf16[3200,3,1024]{0,2,1:T(8,128)(2,1)} copy(bf16[3200,3,1024]{2,0,1:T(8,128)(2,1)} %all-gather.7.cloned.1.call-done) | data formatting | bytes 39321600 | tf_op jit(solution)/shard_map/all_gather | solution.py:32
  186.0 17.9 %fusion.1 = f32[512,3,1024]{2,0,1:T(8,128)} fusion(bf16[3200,3,1024]{0,2,1:T(8,128)(2,1)} %copy.25, bf16[512,3200]{0,1:T(8,128)(2,1)S(1)} %copy-done.2, f32[3200]{0:T(1024)S(1)} %mul.120, f32[512]{0:T(512)S(1)} %add_rsqrt_fusion.2), kind=kOutput, calls=%fused_computation.2 | convolution fusion | flops 10072883200 | bytes 29243904 | tf_op jit(solution)/shard_map/dot_general | solution.py:33
  203.9 1.7 slice.52
  205.7 5.1 %slice_bitcast_fusion = (f32[64,8,8,128]{3,1,2,0:T(8,128)S(1)}, f32[64,8,8,128]{3,1,2,0:T(8,128)}, f32[512]{0:T(512)S(1)}, f32[512,1024]{1,0:T(8,128)}) fusion(f32[512,3,1024]{2,0,1:T(8,128)} %fusion.1), kind=kLoop, calls=%fused_computation.31 | loop fusion | flops 1048064 | bytes 10487808
  211.2 1.8 multiply_reduce_fusion.1
  213.0 4.0 all-reduce.1
  217.0 1.3 copy.36
  218.4 1.3 fusion.32
  219.8 1.5 collective-permute-start
  222.8 0.7 fusion.42
  223.6 1.8 copy.27
  225.3 0.8 copy.31
  226.2 1.1 copy.32
  227.3 5.4 %fusion.23 = f32[8,512,640]{2,1,0:T(8,128)} fusion(bf16[128,8,128]{2,0,1:T(8,128)(2,1)S(1)} %copy.32, bf16[512,8,128]{2,0,1:T(8,128)(2,1)S(1)} %fusion.16, f32[512,8,128]{2,1,0:T(8,128)S(1)} %bitcast.68, f32[8,128]{1,0:T(8,128)S(1)} %bitcast.76, f32[512]{0:T(512)S(1)} %add_rsqrt_fusion), kind=kOutput, calls=%fused_computation.38 | convolution fusion | flops 675282944 | bytes 13899776 | tf_op jit(solution)/shard_map/qhd,khd->hqk/dot_general | solution.py:61
  232.8 15.3 %fusion.44 = (f32[8,512]{1,0:T(8,128)S(1)}, f32[8,512,640]{2,1,0:T(8,128)}) fusion(f32[8,512,640]{2,1,0:T(8,128)} %fusion.23, pred[512,640]{1,0:T(8,128)(4,1)S(1)} %copy-done.4), kind=kOutput, calls=%fused_computation.76 | output fusion | flops 15729279 | bytes 21315584 | tf_op jit(solution)/shard_map/sub | solution.py:67
  248.1 5.9 %fusion.19 = bf16[8,128,512]{2,1,0:T(8,128)(2,1)S(1)} fusion(f32[8,512,640]{2,1,0:T(8,128)} %get-tuple-element.16, f32[8,512]{1,0:T(8,128)S(1)} %get-tuple-element.15, bf16[128,8,128]{0,2,1:T(8,128)(2,1)S(1)} %bitcast.71, bf16[512,8,128]{0,2,1:T(8,128)(2,1)S(1)} %bitcast.69), kind=kOutput, calls=%fused_computation.34 | convolution fusion | flops 679477248 | bytes 12861440 | tf_op jit(solution)/shard_map/hqk,khd->qhd/dot_general | solution.py:69
  254.1 7.8 %convolution_convert_fusion = bf16[512,3200]{0,1:T(8,128)(2,1)} fusion(bf16[1024,3200]{0,1:T(8,128)(2,1)} %all-gather.9.cloned.1.call-done, bf16[512,1024]{0,1:T(8,128)(2,1)S(1)} %bitcast.78), kind=kOutput, calls=%fused_computation.13 | convolution fusion | flops 3357081600 | bytes 10878976 | tf_op jit(solution)/shard_map/dot_general | solution.py:71
  262.5 1.3 reduce-window.6
  264.3 42.3 %reduce-scatter.2.cloned.1.call-done = bf16[512,1600]{0,1:T(8,128)(2,1)} async-done(((bf16[512,3200]{0,1:T(8,128)(2,1)}), bf16[512,1600]{0,1:T(8,128)(2,1)}) %reduce-scatter.2.cloned.1.call-update) | async-done | bytes 1638416 | tf_op jit(solution)/shard_map/reduce_scatter | solution.py:76
  306.6 2.0 add_convert_fusion
  308.6 2.3 copy.33
  311.3 60.6 %scatter_fusion = bf16[16,64,1600]{2,1,0:T(8,128)(2,1)S(1)} fusion(bf16[16,64,1600]{2,1,0:T(8,128)(2,1)S(1)} %broadcast_in_dim.16, s32[512]{0:T(512)S(1)} %bitcast.65, bf16[512,1600]{1,0:T(8,128)(2,1)} %copy.33), kind=kCustom, calls=%fused_computation | custom fusion | bytes 4919296 | tf_op jit(solution)/shard_map/scatter | solution.py:87
  372.0 82.8 %all_to_all.5 = bf16[16,64,1600]{2,1,0:T(8,128)(2,1)S(1)} all-to-all(bf16[16,64,1600]{2,1,0:T(8,128)(2,1)S(1)} %scatter_fusion), channel_id=1, replica_groups=mesh['group'=16,'tp'=2] {'group'}, dimensions={0} | all-to-all | bytes 6553600 | tf_op jit(solution)/shard_map/all_to_all | solution.py:89
  454.8 1.8 copy.55
  (56 shorter events, 4.8 us)
Async XLA Ops:
  6.5 2.4 copy-start.11
  6.5 2.3 copy-start.8
  6.5 3.7 copy-start.10
  6.5 4.0 copy-start.9
  6.5 50.9 %all-gather.5.cloned.1.call-start = ((), (), s32[]{:S(2)}) async-start(), calls=%async_computation.2 | async-start | bytes 4915200 | tf_op jit(solution)/shard_map/all_gather | solution.py:26
  7.3 154.8 %all-gather.7.cloned.1.call-start = ((), (), s32[]{:S(2)}) async-start(), calls=%async_computation.3 | async-start | bytes 20889600 | tf_op jit(solution)/shard_map/all_gather | solution.py:32
  8.0 246.0 %all-gather.9.cloned.1.call-start = ((), (), s32[]{:S(2)}) async-start(), calls=%async_computation.4 | async-start | bytes 6963200 | tf_op jit(solution)/shard_map/all_gather | solution.py:73
  8.8 297.8 %reduce-scatter.2.cloned.1.call-start = ((), (), s32[]{:S(2)}) async-start(), calls=%async_computation.5 | async-start | bytes 4915200 | tf_op jit(solution)/shard_map/reduce_scatter | solution.py:76
  8.9 6.7 %collective-permute-start.1 = (s32[128]{0:T(128)S(1)}, s32[128]{0:T(128)S(1)}, u32[]{:S(2)}, u32[]{:S(2)}) collective-permute-start(s32[128]{0:T(128)S(1)} %dynamic_slice.11), channel_id=1, source_target_pairs={{0,2},{2,0},{4,6},{6,4},{8,10},{10,8},{12,14},{14,12},{16,18},{18,... | collective-permute-start | bytes 1544 | tf_op jit(solution)/shard_map/ppermute | solution.py:15
  60.1 125.9 %copy-start.2 = (bf16[512,3200]{0,1:T(8,128)(2,1)S(1)}, bf16[512,3200]{0,1:T(8,128)(2,1)}, u32[]{:S(2)}) copy-start(bf16[512,3200]{0,1:T(8,128)(2,1)} %all-gather.5.cloned.1.call-done) | copy-start | bytes 9830404
  218.4 2.9 copy-start
  219.8 3.0 collective-permute-start
  227.3 5.4 %copy-start.4 = (pred[512,640]{1,0:T(8,128)(4,1)S(1)}, pred[512,640]{1,0:T(8,128)(4,1)}, u32[]{:S(2)}) copy-start(pred[512,640]{1,0:T(8,128)(4,1)} %broadcast_compare_fusion) | copy-start | bytes 983044
  232.7 15.3 %copy-start.3 = (bf16[512,1,1024]{0,2,1:T(8,128)(2,1)S(1)}, bf16[512,1,1024]{0,2,1:T(8,128)(2,1)}, u32[]{:S(2)}) copy-start(bf16[512,1,1024]{0,2,1:T(8,128)(2,1)} %copy.36) | copy-start | bytes 3145732
  232.7 15.3 %copy-start.5 = (bf16[1,128,1024]{1,2,0:T(8,128)(2,1)S(1)}, bf16[1,128,1024]{1,2,0:T(8,128)(2,1)}, u32[]{:S(2)}) copy-start(bf16[1,128,1024]{1,2,0:T(8,128)(2,1)} %copy.27) | copy-start | bytes 786436
  261.8 0.7 copy-start.6
  261.8 44.7 %copy-start.1 = (bf16[512,1600]{0,1:T(8,128)(2,1)S(1)}, bf16[512,1600]{0,1:T(8,128)(2,1)}, u32[]{:S(2)}) copy-start(bf16[512,1600]{0,1:T(8,128)(2,1)} %param.8) | copy-start | bytes 4915204
  261.9 44.7 %copy-start.7 = (f32[1600]{0:T(1024)S(1)}, f32[1600]{0:T(1024)}, u32[]{:S(2)}) copy-start(f32[1600]{0:T(1024)} %param.13) | copy-start | bytes 19204
Sparse Core Ops, SparseCore 0:
  8.9 48.4 all-gather.4
  59.0 103.0 all-gather.6
  164.4 63.3 all-gather.8
  262.0 44.5 reduce-scatter.1
where the time goes:
time: 466 us; the launch traced here: 463 us
  waiting for transfers between devices  188 us (40%)
  local copies, waits for them, and re-layouts  99.5 us (21%)
  blocking collectives  91.8 us (20%)
  matrix products  37 us (8%)
  other arithmetic  31.2 us (7%)
  between operations  14 us (3%)
    all_gather x1, waiting for transfers between devices, shards(): piece = lax.all_gather(w_qkv, 'group', axis=0, tiled=True)  102 us
    all_to_all x1, blocking collectives, shards(): lax.all_to_all(outbox, 'group', split_axis=0, concat_axis=0, tiled=True)  82.8 us
    scatter x1, local copies, waits for them, and re-layouts, shards(): jnp.zeros((group_count, capacity, feat_local), jnp.bfloat16)  60.6 us
    reduce_scatter x1, waiting for transfers between devices, shards(): lax.psum_scatter(partial_terms.astype(jnp.bfloat16), 'tp', scatter_dimens...  42.3 us
    all_gather x1, waiting for transfers between devices, shards(): lax.all_gather(tokens, 'tp', axis=1, tiled=True)  40.9 us
    all_gather x1, local copies, waits for them, and re-layouts, shards(): piece = lax.all_gather(w_qkv, 'group', axis=0, tiled=True)  24 us
    dot_general x1, matrix products, shards(): jnp.dot(normed, piece.reshape(piece.shape[0], 3 * local_width), preferred...  17.9 us
    sub x1, other arithmetic, shards(): expo = jnp.exp(scores - top)  15.3 us
  transfers between devices with their start and end apart: 6, of which 4 were waited for; matrix products, arithmetic and copies ran while one was open for 20% of the time, Pallas kernels for 0%

commit v1 on v0

v1 whole, which is shorter than its diff:
```python
import math

import jax
import jax.numpy as jnp
from jax import lax
from jax.sharding import PartitionSpec as P

HD = 128
SHARE = 128


def swapped(value, axis, apart):
    mask = 2**apart
    pairs = [(source, source ^ mask) for source in range(lax.axis_size(axis))]
    return lax.ppermute(value, axis, pairs)


def from_next(value, axis):
    count = lax.axis_size(axis)
    return lax.ppermute(value, axis, [((i + 1) % count, i) for i in range(count)])


def shards(tokens, norm_gain, w_qkv, qk_gain, w_out, layer_scale, request, owner):
    rows, feat_local = tokens.shape
    tp_count = lax.axis_size("tp")
    group_count = lax.axis_size("group")
    local_width = w_qkv.shape[2]
    head_count = local_width // HD
    me_tp = lax.axis_index("tp")
    w_k, w_q = (
        lax.all_gather(w_qkv[:, i, :], "group", axis=0, tiled=True) for i in (1, 0)
    )
    whole = jnp.zeros((rows, feat_local * tp_count), jnp.bfloat16)
    gain_all = jnp.zeros((1, feat_local * tp_count), jnp.bfloat16)
    piece, gain = tokens, norm_gain.reshape(1, feat_local)
    for step in range(tp_count):
        at = ((me_tp + step) % tp_count) * feat_local
        whole = lax.dynamic_update_slice(whole, piece, (0, at))
        gain_all = lax.dynamic_update_slice(gain_all, gain, (0, at))
        if step < tp_count - 1:
            piece, gain = from_next(piece, "tp"), from_next(gain, "tp")
    whole, late_v, late_out = lax.optimization_barrier((whole, w_qkv[:, 2, :], w_out))
    w_v = lax.all_gather(late_v, "group", axis=0, tiled=True)
    per = group_count // tp_count
    pairs = []
    for g in range(group_count):
        for b in range(tp_count):
            t, j = g // per, g % per
            to_g = ((b - t) % tp_count) * per + j
            pairs.append((g * tp_count + b, to_g * tp_count + t))
    w_piece = lax.ppermute(late_out.T, ("group", "tp"), pairs)
    w_o = lax.all_gather(w_piece, "group", axis=0, tiled=True)
    w_o = w_o.reshape(tp_count, feat_local, local_width)
    xwide = whole.astype(jnp.float32)
    stat = jnp.mean(xwide * xwide, axis=-1, keepdims=True)
    normed = (xwide * lax.rsqrt(stat + 1e-06) * gain_all.astype(jnp.float32)).astype(jnp.bfloat16)
    key_rows = jnp.dot(normed, w_k, preferred_element_type=jnp.float32)
    query = jnp.dot(normed, w_q, preferred_element_type=jnp.float32)
    qsum, ksum = lax.psum(
        (jnp.sum(query * query, axis=-1), jnp.sum(key_rows * key_rows, axis=-1)), "tp"
    )
    total_width = local_width * tp_count
    qnorm = (query * lax.rsqrt(qsum / total_width + 1e-06)[:, None] * qk_gain[0]).astype(
        jnp.bfloat16
    )
    knorm = (key_rows * lax.rsqrt(ksum / total_width + 1e-06)[:, None] * qk_gain[1]).astype(
        jnp.bfloat16
    )
    parity = lax.axis_index("group") % 2
    seam = jnp.where(parity == 0, rows - SHARE, 0).astype(jnp.int32)
    key_window = lax.dynamic_slice_in_dim(knorm, seam, SHARE, 0)
    id_window = lax.dynamic_slice_in_dim(request, seam, SHARE, 0)
    paired_key, paired_ids = swapped((key_window, id_window), "group", 0)
    all_keys = jnp.concatenate([knorm, paired_key], axis=0)
    all_ids = jnp.concatenate([request, paired_ids], axis=0)
    qheads = qnorm.reshape(rows, head_count, HD)
    kheads = all_keys.reshape(rows + SHARE, head_count, HD)
    scores = jnp.einsum(
        "qhd,khd->hqk", qheads, kheads, preferred_element_type=jnp.float32
    ) / math.sqrt(HD)
    same = request[:, None] == all_ids[None, :]
    scores = jnp.where(same[None], scores, -jnp.inf)
    top = jnp.max(scores, axis=-1, keepdims=True)
    expo = jnp.exp(scores - top)
    probs = (expo / jnp.sum(expo, axis=-1, keepdims=True)).astype(jnp.bfloat16)

    value = jnp.dot(normed, w_v, preferred_element_type=jnp.float32).astype(jnp.bfloat16)
    value_window = lax.dynamic_slice_in_dim(value, seam, SHARE, 0)
    all_values = jnp.concatenate([value, swapped(value_window, "group", 0)], axis=0)
    vheads = all_values.reshape(rows + SHARE, head_count, HD)
    attended = jnp.einsum("hqk,khd->qhd", probs, vheads, preferred_element_type=jnp.float32)
    attended = attended.astype(jnp.bfloat16).reshape(rows, local_width)

    branch = jnp.zeros((rows, feat_local), jnp.float32)
    for step in range(tp_count):
        onward = from_next(attended, "tp") if step < tp_count - 1 else None
        part = lax.dot_general(
            attended, w_o[step], (((1,), (1,)), ((), ())), preferred_element_type=jnp.float32
        )
        branch = branch + part.astype(jnp.bfloat16).astype(jnp.float32)
        attended = onward
    mixed = (tokens.astype(jnp.float32) + layer_scale * branch).astype(jnp.bfloat16)

    capacity = max(2, 2 * rows // group_count)
    target = owner[:, 0]
    onehot = (target[:, None] == jnp.arange(group_count, dtype=jnp.int32)[None, :]).astype(
        jnp.int32
    )
    slot = jnp.sum((jnp.cumsum(onehot, axis=0) - onehot) * onehot, axis=-1)
    place = target * capacity + slot
    select = (
        jnp.arange(group_count * capacity, dtype=jnp.int32)[:, None] == place[None, :]
    ).astype(jnp.bfloat16)
    outbox = jnp.dot(select, mixed, preferred_element_type=jnp.float32).astype(jnp.bfloat16)
    outbox = outbox.reshape(group_count, capacity, feat_local)
    inbox = lax.all_to_all(outbox, "group", split_axis=0, concat_axis=0, tiled=True)
    return inbox[None]


def solution(mesh):
    in_specs = (
        P("group", "tp"),
        P("tp"),
        P("group", None, "tp"),
        P(None, "tp"),
        P("tp", "group"),
        P("tp"),
        P("group"),
        P("group", None),
    )
    out_specs = P("group", None, None, "tp")
    return jax.shard_map(shards, mesh=mesh, in_specs=in_specs, out_specs=out_specs, check_vma=False)
```

time: 466 us -> 389 us (0.83)
  local copies, waits for them, and re-layouts: 99.5 us -> 13.7 us
  starting transfers between devices: 1.72 us -> 46.6 us
  waiting for transfers between devices: 188 us -> 162 us
  matrix products: 37 us -> 47.7 us
  other arithmetic: 31.2 us -> 20.6 us
  blocking collectives: 91.8 us -> 84.5 us
    scatter x1 -> x0, local copies, waits for them, and re-layouts: 60.6 us -> none  [shards(): jnp.zeros((group_count, capacity, feat_local), jnp.bfloat16)]
    ppermute x0 -> x4, starting transfers between devices: none -> 44.1 us  [the longest x3 39.2 us: from_next(): lax.ppermute(value, axis, [((i + 1) % count, i) for i in range(count)])]
    reduce_scatter x1 -> x0, waiting for transfers between devices: 42.3 us -> none  [shards(): lax.psum_scatter(partial_terms.astype(jnp.bfloat16), 'tp', scatter_dimens...]
    ppermute x0 -> x4, waiting for transfers between devices: none -> 34 us  [the longest x3 34 us: from_next(): lax.ppermute(value, axis, [((i + 1) % count, i) for i in range(count)])]
    all_gather x1 -> x0, local copies, waits for them, and re-layouts: 24 us -> none  [shards(): piece = lax.all_gather(w_qkv, 'group', axis=0, tiled=True)]
    all_gather x3 -> x4, waiting for transfers between devices: 143 us -> 127 us  [the longest x2 53.1 us: shards(): lax.all_gather(w_qkv[:, i, :], 'group', axis=0, tiled=True)]
    dot_general x2 -> x5, matrix products: 25.7 us -> 36.2 us  [the longest x1 8.52 us: shards(): jnp.dot(select, mixed, preferred_element_type=jnp.float32)]
    unnamed x1 -> x0, other arithmetic: 5.06 us -> none
  transfers between devices with their start and end apart: 6 -> 11, of which waited for: 4 -> 6; matrix products, arithmetic and copies ran while one was open for 20% -> 17% of each run, Pallas kernels for 0% -> 0%
where the time goes in v1:
time: 389 us
  waiting for transfers between devices  162 us (42%)
  blocking collectives  84.5 us (22%)
  matrix products  47.7 us (12%)
  starting transfers between devices  46.6 us (12%)
  other arithmetic  20.6 us (5%)
  local copies, waits for them, and re-layouts  13.7 us (4%)
  between operations  13.3 us (3%)
    all_to_all x1, blocking collectives, shards(): lax.all_to_all(outbox, 'group', split_axis=0, concat_axis=0, tiled=True)  80.1 us
    all_gather x2, waiting for transfers between devices, shards(): lax.all_gather(w_qkv[:, i, :], 'group', axis=0, tiled=True)  53.1 us
    all_gather x1, waiting for transfers between devices, shards(): w_v = lax.all_gather(late_v, 'group', axis=0, tiled=True)  42.1 us
    ppermute x3, starting transfers between devices, from_next(): lax.ppermute(value, axis, [((i + 1) % count, i) for i in range(count)])  39.2 us
    ppermute x3, waiting for transfers between devices, from_next(): lax.ppermute(value, axis, [((i + 1) % count, i) for i in range(count)])  34 us
    all_gather x1, waiting for transfers between devices, shards(): w_o = lax.all_gather(w_piece, 'group', axis=0, tiled=True)  31.7 us
    sub x1, other arithmetic, shards(): expo = jnp.exp(scores - top)  15.4 us
    dot_general x1, matrix products, shards(): jnp.dot(select, mixed, preferred_element_type=jnp.float32)  8.52 us
  transfers between devices with their start and end apart: 11, of which 6 were waited for; matrix products, arithmetic and copies ran while one was open for 17% of the time, Pallas kernels for 0%

profile of v1, /device:TPU:1, one launch (start us, length us, event | category | flops | bytes accessed | tf_op | source)
XLA Modules:
  0.0 388.7 jit_solution(6893190634772849694)
XLA Ops:
  6.5 2.3 fusion.44
  8.9 0.7 all-gather.11.cloned.1.call-update
  9.7 2.1 collective-permute-start
  12.0 1.6 constant_dynamic-update-slice_fusion.1
  13.6 34.0 %collective-permute-done = bf16[512,1600]{0,1:T(8,128)(2,1)} collective-permute-done((bf16[512,1600]{0,1:T(8,128)(2,1)}, bf16[512,1600]{0,1:T(8,128)(2,1)}, u32[]{:S(2)}, u32[]{:S(2)}) %collective-permute-start) | collective-permute-done | bytes 1638432 | tf_op jit(solution)/shard_map/ppermute | solution.py:20
  47.6 1.6 constant_dynamic-update-slice_fusion
  49.3 4.9 %collective-permute-start.5 = (bf16[200,1024]{1,0:T(8,128)(2,1)}, bf16[200,1024]{1,0:T(8,128)(2,1)}, u32[]{:S(2)}, u32[]{:S(2)}) collective-permute-start(bf16[200,1024]{1,0:T(8,128)(2,1)} %bitcast.70), channel_id=1, source_target_pairs={{0,0},{1,16},{2,2},{3,18},{4,4},{5,20},{6,6},{7,22},{8,8},{9,24},{... | collective-permute-start | bytes 1228808 | tf_op jit(solution)/shard_map/ppermute | solution.py:51
  54.2 35.8 %collective-permute-start.1 = (bf16[1,1600]{1,0:T(2,128)(2,1)S(1)}, bf16[1,1600]{1,0:T(2,128)(2,1)S(1)}, u32[]{:S(2)}, u32[]{:S(2)}) collective-permute-start(bf16[1,1600]{1,0:T(2,128)(2,1)S(1)} %reshape.93), channel_id=1, source_target_pairs={{1,0},{0,1},{3,2},{2,3},{5,4},{4,5},{7,6},{6,7},{9,8},{8,9},{11,10... | collective-permute-start | bytes 9608 | tf_op jit(solution)/shard_map/ppermute | solution.py:20
  90.1 0.9 collective-permute-start.3
  91.4 0.5 collective-permute-done.3
  92.2 0.8 fusion.2
  93.0 8.0 %multiply_reduce_fusion = (f32[512]{0:T(512)S(1)}, f32[512,1024]{1,0:T(8,128)}) fusion(bf16[3200,1,1024]{2,0,1:T(8,128)(2,1)} %all-gather.13.cloned.1.call-done, bf16[512,3200]{0,1:T(8,128)(2,1)S(1)} %constant_dynamic-update-slice_fusion, f32[3200]{0:T(1024)S(1)} %mul.106, f32[512]{0:T(512)S(1)} %add_rsqrt_fusion.2), kind=kOutput, calls=%fused_computation.27 | convolution fusion | flops 3363044864 | bytes 11944448 | tf_op jit(solution)/shard_map/dot_general | solution.py:57
  101.0 53.1 %all-gather.11.cloned.1.call-done = bf16[3200,1,1024]{2,0,1:T(8,128)(2,1)} async-done(((bf16[200,1,1024]{2,0,1:T(8,128)(2,1)}), bf16[3200,1,1024]{2,0,1:T(8,128)(2,1)}) %all-gather.11.cloned.1.call-update) | async-done | bytes 6553616 | tf_op jit(solution)/shard_map/all_gather | solution.py:31
  154.1 8.0 %multiply_reduce_fusion.1 = (f32[512]{0:T(512)S(1)}, f32[512,1024]{1,0:T(8,128)}) fusion(bf16[3200,1,1024]{2,0,1:T(8,128)(2,1)} %all-gather.11.cloned.1.call-done, bf16[512,3200]{0,1:T(8,128)(2,1)S(1)} %constant_dynamic-update-slice_fusion, f32[3200]{0:T(1024)S(1)} %mul.106, f32[512]{0:T(512)S(1)} %add_rsqrt_fusion.2), kind=kOutput, calls=%fused_computation.29 | convolution fusion | flops 3363044864 | bytes 11944448 | tf_op jit(solution)/shard_map/dot_general | solution.py:58
  162.1 4.3 %all-reduce = (f32[512]{0:T(512)S(1)}, f32[512]{0:T(512)S(1)}) all-reduce(f32[512]{0:T(512)S(1)} %get-tuple-element.18, f32[512]{0:T(512)S(1)} %get-tuple-element.20), channel_id=1, replica_groups=mesh['group'=16,'tp'=2] {'tp'}, use_global_device_ids=true, to_apply=%region_7.8 | all-reduce | flops 1024 | bytes 8192 | tf_op jit(solution)/shard_map/psum | solution.py:59
  166.4 2.0 multiply_convert_fusion
  168.5 1.1 collective-permute-start.4
  169.5 1.0 broadcast_compare_fusion
  170.7 5.6 %fusion.26 = f32[8,512,640]{2,1,0:T(8,128)} fusion(bf16[128,1024]{1,0:T(8,128)(2,1)S(1)} %collective-permute-done.4, bf16[512,1024]{1,0:T(8,128)(2,1)S(1)} %multiply_convert_fusion, f32[512,1024]{1,0:T(8,128)S(1)} %copy-done, f32[1024]{0:T(1024)S(1)} %bitcast.66, f32[512]{0:T(512)S(1)} %add_rsqrt_fusion.1), kind=kOutput, calls=%fused_computation.33 | convolution fusion | flops 675282944 | bytes 13899776 | tf_op jit(solution)/shard_map/qhd,khd->hqk/dot_general | solution.py:78
  176.3 42.1 %all-gather.7.cloned.1.call-done = bf16[3200,1024]{1,0:T(8,128)(2,1)} async-done(((bf16[200,1024]{1,0:T(8,128)(2,1)}), bf16[3200,1024]{1,0:T(8,128)(2,1)}) %all-gather.7.cloned.1.call-update) | async-done | bytes 6553616 | tf_op jit(solution)/shard_map/all_gather | solution.py:43
  218.3 6.7 %convolution_convert_fusion.1 = bf16[512,1024]{1,0:T(8,128)(2,1)S(1)} fusion(bf16[3200,1024]{1,0:T(8,128)(2,1)} %all-gather.7.cloned.1.call-done, bf16[512,3200]{0,1:T(8,128)(2,1)S(1)} %constant_dynamic-update-slice_fusion, f32[3200]{0:T(1024)S(1)} %mul.106, f32[512]{0:T(512)S(1)} %add_rsqrt_fusion.2), kind=kOutput, calls=%fused_computation.32 | convolution fusion | flops 3362521088 | bytes 10893824 | tf_op jit(solution)/shard_map/dot_general | solution.py:87
  225.4 15.4 %fusion.46 = (f32[8,512]{1,0:T(8,128)S(1)}, f32[8,512,640]{2,1,0:T(8,128)}) fusion(f32[8,512,640]{2,1,0:T(8,128)} %fusion.26, pred[512,640]{1,0:T(8,128)(4,1)S(1)} %copy-done.1), kind=kOutput, calls=%fused_computation.66 | output fusion | flops 15729279 | bytes 21315584 | tf_op jit(solution)/shard_map/sub | solution.py:84
  240.9 1.0 copy.18
  241.9 6.0 %fusion.25 = bf16[8,128,512]{2,1,0:T(8,128)(2,1)S(1)} fusion(bf16[640,8,128]{0,2,1:T(8,128)(2,1)S(1)} %bitcast.62, f32[8,512,640]{2,1,0:T(8,128)} %get-tuple-element.23, f32[8,512]{1,0:T(8,128)S(1)} %get-tuple-element.22), kind=kOutput, calls=%fused_computation.31 | convolution fusion | flops 676855808 | bytes 12861440 | tf_op jit(solution)/shard_map/hqk,khd->qhd/dot_general | solution.py:91
  247.9 1.3 collective-permute-start.6
  249.2 1.2 reduce-window.6
  250.7 31.7 %all-gather.9.cloned.1.call-done = bf16[3200,1024]{1,0:T(8,128)(2,1)} async-done(((bf16[200,1024]{1,0:T(8,128)(2,1)}), bf16[3200,1024]{1,0:T(8,128)(2,1)}) %all-gather.9.cloned.1.call-update) | async-done | bytes 6553616 | tf_op jit(solution)/shard_map/all_gather | solution.py:52
  282.4 5.0 %fusion.17 = bf16[512,1600]{0,1:T(8,128)(2,1)} fusion(bf16[512,1024]{0,1:T(8,128)(2,1)S(1)} %bitcast.69, bf16[3200,1024]{1,0:T(8,128)(2,1)} %all-gather.9.cloned.1.call-done), kind=kOutput, calls=%fused_computation.24 | convolution fusion | flops 1678540800 | bytes 5963776 | tf_op jit(solution)/shard_map/dot_general | solution.py:97
  287.4 8.5 %convolution_convert_fusion = bf16[1024,1600]{0,1:T(8,128)(2,1)} fusion(s32[512]{0:T(512)S(1)} %multiply_add_fusion, bf16[512,1600]{0,1:T(8,128)(2,1)} %fusion.17, bf16[512,1600]{0,1:T(8,128)(2,1)} %param.8, bf16[512,1024]{0,1:T(8,128)(2,1)S(1)} %collective-permute-done.6, bf16[3200,1024]{1,0:T(8,128)(2,1)} %all-gather.9.cloned.1.call-done, ...), kind=kOutput, calls=%fused_computation.18 | convolution fusion | flops 3364159488 | bytes 10887424 | tf_op jit(solution)/shard_map/dot_general | solution.py:114
  295.9 4.3 %copy.17 = bf16[1024,1600]{1,0:T(8,128)(2,1)S(1)} copy(bf16[1024,1600]{0,1:T(8,128)(2,1)} %convolution_convert_fusion) | data formatting | bytes 6553600 | tf_op jit(solution)/shard_map/convert_element_type | solution.py:114
  300.3 80.1 %all_to_all.5 = bf16[16,64,1600]{2,1,0:T(8,128)(2,1)S(1)} all-to-all(bf16[16,64,1600]{2,1,0:T(8,128)(2,1)S(1)} %bitcast.60), channel_id=1, replica_groups=mesh['group'=16,'tp'=2] {'group'}, dimensions={0} | all-to-all | bytes 6553600 | tf_op jit(solution)/shard_map/all_to_all | solution.py:116
  380.4 1.8 copy.36
  (50 shorter events, 2.2 us)
Async XLA Ops:
  6.5 86.5 %all-gather.13.cloned.1.call-start = ((), (), s32[]{:S(2)}) async-start(), calls=%async_computation.4 | async-start | bytes 6963200 | tf_op jit(solution)/shard_map/all_gather | solution.py:31
  8.9 145.2 %all-gather.11.cloned.1.call-start = ((), (), s32[]{:S(2)}) async-start(), calls=%async_computation.3 | async-start | bytes 6963200 | tf_op jit(solution)/shard_map/all_gather | solution.py:31
  9.6 208.7 %all-gather.7.cloned.1.call-start = ((), (), s32[]{:S(2)}) async-start(), calls=%async_computation.1 | async-start | bytes 6963200 | tf_op jit(solution)/shard_map/all_gather | solution.py:43
  9.7 38.0 %collective-permute-start = (bf16[512,1600]{0,1:T(8,128)(2,1)}, bf16[512,1600]{0,1:T(8,128)(2,1)}, u32[]{:S(2)}, u32[]{:S(2)}) collective-permute-start(bf16[512,1600]{0,1:T(8,128)(2,1)} %param.8), channel_id=1, source_target_pairs={{1,0},{0,1},{3,2},{2,3},{5,4},{4,5},{7,6},{6,7},{9,8},{8,9},{11,10... | collective-permute-start | bytes 4915208 | tf_op jit(solution)/shard_map/ppermute | solution.py:20
  12.0 42.2 %copy-start.3 = (bf16[1600]{0:T(1024)(128)(2,1)S(1)}, bf16[1600]{0:T(1024)(128)(2,1)}, u32[]{:S(2)}) copy-start(bf16[1600]{0:T(1024)(128)(2,1)} %param.9) | copy-start | bytes 9604
  12.0 78.0 %copy-start.4 = (s32[512]{0:T(512)S(1)}, s32[512]{0:T(512)}, u32[]{:S(2)}) copy-start(s32[512]{0:T(512)} %param.14) | copy-start | bytes 6148
  12.0 79.0 %copy-start.5 = (f32[2,1024]{1,0:T(2,128)S(1)}, f32[2,1024]{1,0:T(2,128)}, u32[]{:S(2)}) copy-start(f32[2,1024]{1,0:T(2,128)} %param.11) | copy-start | bytes 24580
  49.2 233.2 %all-gather.9.cloned.1.call-start = ((), (), s32[]{:S(2)}) async-start(), calls=%async_computation.2 | async-start | bytes 6963200 | tf_op jit(solution)/shard_map/all_gather | solution.py:52
  49.3 4.9 %collective-permute-start.5 = (bf16[200,1024]{1,0:T(8,128)(2,1)}, bf16[200,1024]{1,0:T(8,128)(2,1)}, u32[]{:S(2)}, u32[]{:S(2)}) collective-permute-start(bf16[200,1024]{1,0:T(8,128)(2,1)} %bitcast.70), channel_id=1, source_target_pairs={{0,0},{1,16},{2,2},{3,18},{4,4},{5,20},{6,6},{7,22},{8,8},{9,24},{... | collective-permute-start | bytes 1228808 | tf_op jit(solution)/shard_map/ppermute | solution.py:51
  54.2 37.6 %collective-permute-start.1 = (bf16[1,1600]{1,0:T(2,128)(2,1)S(1)}, bf16[1,1600]{1,0:T(2,128)(2,1)S(1)}, u32[]{:S(2)}, u32[]{:S(2)}) collective-permute-start(bf16[1,1600]{1,0:T(2,128)(2,1)S(1)} %reshape.93), channel_id=1, source_target_pairs={{1,0},{0,1},{3,2},{2,3},{5,4},{4,5},{7,6},{6,7},{9,8},{8,9},{11,10... | collective-permute-start | bytes 9608 | tf_op jit(solution)/shard_map/ppermute | solution.py:20
  90.1 1.8 collective-permute-start.3
  166.4 4.3 %copy-start = (f32[512,1024]{1,0:T(8,128)S(1)}, f32[512,1024]{1,0:T(8,128)}, u32[]{:S(2)}) copy-start(f32[512,1024]{1,0:T(8,128)} %get-tuple-element.21) | copy-start | bytes 6291460
  168.5 2.2 collective-permute-start.4
  218.3 7.1 %copy-start.1 = (pred[512,640]{1,0:T(8,128)(4,1)S(1)}, pred[512,640]{1,0:T(8,128)(4,1)}, u32[]{:S(2)}) copy-start(pred[512,640]{1,0:T(8,128)(4,1)} %broadcast_compare_fusion) | copy-start | bytes 983044
  225.1 15.7 %collective-permute-start.2 = (bf16[128,1024]{1,0:T(8,128)(2,1)S(1)}, bf16[128,1024]{1,0:T(8,128)(2,1)S(1)}, u32[]{:S(2)}, u32[]{:S(2)}) collective-permute-start(bf16[128,1024]{1,0:T(8,128)(2,1)S(1)} %constant_dynamic-slice_fusion.1), channel_id=1, source_target_pairs={{0,2},{2,0},{4,6},{6,4},{8,10},{10,8},{12,14},{14,12},{16,18},{18,... | collective-permute-start | bytes 786440 | tf_op jit(solution)/shard_map/ppermute | solution.py:15
  241.9 7.3 %copy-start.2 = (s32[512,1]{0,1:T(1,128)S(1)}, s32[512,1]{0,1:T(1,128)}, u32[]{:S(2)}) copy-start(s32[512,1]{0,1:T(1,128)} %param.15) | copy-start | bytes 6148
  247.9 39.5 %collective-permute-start.6 = (bf16[512,1024]{0,1:T(8,128)(2,1)S(1)}, bf16[512,1024]{0,1:T(8,128)(2,1)S(1)}, u32[]{:S(2)}, u32[]{:S(2)}) collective-permute-start(bf16[512,1024]{0,1:T(8,128)(2,1)S(1)} %bitcast.68), channel_id=1, source_target_pairs={{1,0},{0,1},{3,2},{2,3},{5,4},{4,5},{7,6},{6,7},{9,8},{8,9},{11,10... | collective-permute-start | bytes 3145736 | tf_op jit(solution)/shard_map/ppermute | solution.py:20
  250.7 36.7 %copy-start.6 = (f32[1600]{0:T(1024)S(1)}, f32[1600]{0:T(1024)}, u32[]{:S(2)}) copy-start(f32[1600]{0:T(1024)} %param.13) | copy-start | bytes 19204
Sparse Core Ops, SparseCore 0:
  9.6 65.8 all-gather.12
  77.9 76.1 all-gather.10
  156.3 61.9 all-gather.6
  220.5 61.8 all-gather.8

commit v2 on v1

--- a/solution.py
+++ b/solution.py
@@ -27,8 +27,8 @@
     local_width = w_qkv.shape[2]
     head_count = local_width // HD
     me_tp = lax.axis_index("tp")
-    w_k, w_q = (
-        lax.all_gather(w_qkv[:, i, :], "group", axis=0, tiled=True) for i in (1, 0)
+    w_all = lax.all_gather(
+        w_qkv.reshape(w_qkv.shape[0], 3 * local_width), "group", axis=0, tiled=True
     )
     whole = jnp.zeros((rows, feat_local * tp_count), jnp.bfloat16)
     gain_all = jnp.zeros((1, feat_local * tp_count), jnp.bfloat16)
@@ -39,8 +39,7 @@
         gain_all = lax.dynamic_update_slice(gain_all, gain, (0, at))
         if step < tp_count - 1:
             piece, gain = from_next(piece, "tp"), from_next(gain, "tp")
-    whole, late_v, late_out = lax.optimization_barrier((whole, w_qkv[:, 2, :], w_out))
-    w_v = lax.all_gather(late_v, "group", axis=0, tiled=True)
+    whole, late_out = lax.optimization_barrier((whole, w_out))
     per = group_count // tp_count
     pairs = []
     for g in range(group_count):
@@ -54,8 +53,10 @@
     xwide = whole.astype(jnp.float32)
     stat = jnp.mean(xwide * xwide, axis=-1, keepdims=True)
     normed = (xwide * lax.rsqrt(stat + 1e-06) * gain_all.astype(jnp.float32)).astype(jnp.bfloat16)
-    key_rows = jnp.dot(normed, w_k, preferred_element_type=jnp.float32)
-    query = jnp.dot(normed, w_q, preferred_element_type=jnp.float32)
+    qkv = jnp.dot(normed, w_all, preferred_element_type=jnp.float32)
+    query = qkv[:, :local_width]
+    key_rows = qkv[:, local_width : 2 * local_width]
+    value = qkv[:, 2 * local_width :].astype(jnp.bfloat16)
     qsum, ksum = lax.psum(
         (jnp.sum(query * query, axis=-1), jnp.sum(key_rows * key_rows, axis=-1)), "tp"
     )
@@ -84,7 +85,6 @@
     expo = jnp.exp(scores - top)
     probs = (expo / jnp.sum(expo, axis=-1, keepdims=True)).astype(jnp.bfloat16)
 
-    value = jnp.dot(normed, w_v, preferred_element_type=jnp.float32).astype(jnp.bfloat16)
     value_window = lax.dynamic_slice_in_dim(value, seam, SHARE, 0)
     all_values = jnp.concatenate([value, swapped(value_window, "group", 0)], axis=0)
     vheads = all_values.reshape(rows + SHARE, head_count, HD)

time: 389 us -> 317 us (0.81)
  waiting for transfers between devices: 162 us -> 80.1 us
  blocking collectives: 84.5 us -> 102 us
  matrix products: 47.7 us -> 40.3 us
  starting transfers between devices: 46.6 us -> 39.9 us
    all_gather x3 -> x1, waiting for transfers between devices: 95.2 us -> 28.8 us  [shards(): lax.all_gather(w_qkv.reshape(w_qkv.shape[0], 3 * local_width), 'group', a...]
    all_gather x1, waiting for transfers between devices: 31.7 us -> 10.2 us  [shards(): w_o = lax.all_gather(w_piece, 'group', axis=0, tiled=True)]
    psum x1, blocking collectives: 4.35 us -> 14.3 us  [shards(): lax.psum((jnp.sum(query * query, axis=-1), jnp.sum(key_rows * key_rows, a...]
    dot_general x3 -> x1, matrix products: 22.7 us -> 14.3 us  [shards(): qkv = jnp.dot(normed, w_all, preferred_element_type=jnp.float32)]
    all_to_all x1, blocking collectives: 80.1 us -> 87.3 us  [shards(): lax.all_to_all(outbox, 'group', split_axis=0, concat_axis=0, tiled=True)]
    ppermute x3, waiting for transfers between devices: 34 us -> 40.6 us  [from_next(): lax.ppermute(value, axis, [((i + 1) % count, i) for i in range(count)])]
    ppermute x3, starting transfers between devices: 39.2 us -> 35.1 us  [from_next(): lax.ppermute(value, axis, [((i + 1) % count, i) for i in range(count)])]
  transfers between devices with their start and end apart: 11 -> 9, of which waited for: 6 -> 5; matrix products, arithmetic and copies ran while one was open for 17% -> 20% of each run, Pallas kernels for 0% -> 0%
where the time goes in v2:
time: 317 us
  blocking collectives  102 us (32%)
  waiting for transfers between devices  80.1 us (25%)
  matrix products  40.3 us (13%)
  starting transfers between devices  39.9 us (13%)
  other arithmetic  24.4 us (8%)
  local copies, waits for them, and re-layouts  17 us (5%)
  between operations  13.6 us (4%)
    all_to_all x1, blocking collectives, shards(): lax.all_to_all(outbox, 'group', split_axis=0, concat_axis=0, tiled=True)  87.3 us
    ppermute x3, waiting for transfers between devices, from_next(): lax.ppermute(value, axis, [((i + 1) % count, i) for i in range(count)])  40.6 us
    ppermute x3, starting transfers between devices, from_next(): lax.ppermute(value, axis, [((i + 1) % count, i) for i in range(count)])  35.1 us
    all_gather x1, waiting for transfers between devices, shards(): lax.all_gather(w_qkv.reshape(w_qkv.shape[0], 3 * local_width), 'group', a...  28.8 us
    sub x1, other arithmetic, shards(): expo = jnp.exp(scores - top)  16 us
    psum x1, blocking collectives, shards(): lax.psum((jnp.sum(query * query, axis=-1), jnp.sum(key_rows * key_rows, a...  14.3 us
    dot_general x1, matrix products, shards(): qkv = jnp.dot(normed, w_all, preferred_element_type=jnp.float32)  14.3 us
    all_gather x1, waiting for transfers between devices, shards(): w_o = lax.all_gather(w_piece, 'group', axis=0, tiled=True)  10.2 us
  transfers between devices with their start and end apart: 9, of which 5 were waited for; matrix products, arithmetic and copies ran while one was open for 20% of the time, Pallas kernels for 0%

profile of v2, /device:TPU:1, one launch (start us, length us, event | category | flops | bytes accessed | tf_op | source)
XLA Modules:
  0.0 316.9 jit_solution(11441685035728626753)
XLA Ops:
  6.5 2.4 copy.23
  9.0 2.1 collective-permute-start
  11.4 1.6 constant_dynamic-update-slice_fusion.1
  13.0 33.9 %collective-permute-done = bf16[512,1600]{0,1:T(8,128)(2,1)} collective-permute-done((bf16[512,1600]{0,1:T(8,128)(2,1)}, bf16[512,1600]{0,1:T(8,128)(2,1)}, u32[]{:S(2)}, u32[]{:S(2)}) %collective-permute-start) | collective-permute-done | bytes 1638432 | tf_op jit(solution)/shard_map/ppermute | solution.py:20
  47.0 1.6 constant_dynamic-update-slice_fusion
  48.6 1.4 collective-permute-start.5
  50.1 31.1 %collective-permute-start.1 = (bf16[1,1600]{1,0:T(2,128)(2,1)S(1)}, bf16[1,1600]{1,0:T(2,128)(2,1)S(1)}, u32[]{:S(2)}, u32[]{:S(2)}) collective-permute-start(bf16[1,1600]{1,0:T(2,128)(2,1)S(1)} %reshape.96), channel_id=1, source_target_pairs={{1,0},{0,1},{3,2},{2,3},{5,4},{4,5},{7,6},{6,7},{9,8},{8,9},{11,10... | collective-permute-start | bytes 9608 | tf_op jit(solution)/shard_map/ppermute | solution.py:20
  81.3 2.3 collective-permute-start.3
  83.9 0.5 collective-permute-done.3
  84.8 0.8 fusion.2
  85.5 28.8 %all-gather.3.cloned.1.call-done = bf16[3200,3072]{1,0:T(8,128)(2,1)} async-done(((bf16[200,3072]{1,0:T(8,128)(2,1)}), bf16[3200,3072]{1,0:T(8,128)(2,1)}) %all-gather.3.cloned.1.call-update) | async-done | bytes 19660816 | tf_op jit(solution)/shard_map/all_gather | solution.py:30
  114.3 14.3 %fusion.9 = f32[512,3072]{1,0:T(8,128)S(1)} fusion(bf16[3200,3072]{1,0:T(8,128)(2,1)} %all-gather.3.cloned.1.call-done, bf16[512,3200]{0,1:T(8,128)(2,1)S(1)} %constant_dynamic-update-slice_fusion, f32[3200]{0:T(1024)S(1)} %mul.106, f32[512]{0:T(512)S(1)} %add_rsqrt_fusion.2), kind=kOutput, calls=%fused_computation.15 | convolution fusion | flops 10072883200 | bytes 29243904 | tf_op jit(solution)/shard_map/dot_general | solution.py:56
  129.5 1.8 copy-done
  131.3 14.3 %all-reduce = (f32[512]{0:T(512)S(1)}, f32[512]{0:T(512)S(1)}) all-reduce(f32[512]{0:T(512)S(1)} %get-tuple-element.10, f32[512]{0:T(512)S(1)} %get-tuple-element.9), channel_id=1, replica_groups=mesh['group'=16,'tp'=2] {'tp'}, use_global_device_ids=true, to_apply=%region_7.8 | all-reduce | flops 1024 | bytes 8192 | tf_op jit(solution)/shard_map/psum | solution.py:60
  145.6 3.7 %fusion.29 = (bf16[64,8,8,128]{3,2,1,0:T(8,128)(2,1)}, bf16[512,1024]{1,0:T(8,128)(2,1)S(1)}) fusion(f32[512,3072]{1,0:T(8,128)} %copy-done, f32[1024]{0:T(1024)S(1)} %bitcast.56, f32[512]{0:T(512)S(1)} %get-tuple-element.20, f32[1024]{0:T(1024)S(1)} %bitcast.57, f32[512]{0:T(512)S(1)} %get-tuple-element.19), kind=kLoop, calls=%fused_computation.37 | loop fusion | flops 3145728 | bytes 6303744
  149.3 0.7 constant_dynamic-slice_fusion
  150.0 0.7 collective-permute-start.4
  150.7 1.0 broadcast_compare_fusion
  151.7 1.0 pad_maximum_fusion
  152.8 1.4 copy.19
  154.2 6.5 %fusion.26 = f32[8,512,640]{2,1,0:T(8,128)} fusion(bf16[64,8,8,128]{3,2,1,0:T(8,128)(2,1)S(1)} %copy-done.1, bf16[128,1024]{1,0:T(8,128)(2,1)} %collective-permute-done.4, bf16[512,1024]{1,0:T(8,128)(2,1)S(1)} %get-tuple-element.14), kind=kOutput, calls=%fused_computation.32 | convolution fusion | flops 673710080 | bytes 12845056 | tf_op jit(solution)/shard_map/qhd,khd->hqk/dot_general | solution.py:79
  160.8 16.0 %fusion.42 = (f32[8,512]{1,0:T(8,128)S(1)}, f32[8,512,640]{2,1,0:T(8,128)}) fusion(f32[8,512,640]{2,1,0:T(8,128)} %fusion.26, pred[512,640]{1,0:T(8,128)(4,1)S(1)} %copy-done.3), kind=kOutput, calls=%fused_computation.63 | output fusion | flops 15729279 | bytes 21315584 | tf_op jit(solution)/shard_map/sub | solution.py:85
  176.8 6.0 %fusion.25 = bf16[8,128,512]{2,1,0:T(8,128)(2,1)S(1)} fusion(bf16[640,8,128]{0,2,1:T(8,128)(2,1)S(1)} %bitcast.51, f32[8,512,640]{2,1,0:T(8,128)} %get-tuple-element.18, f32[8,512]{1,0:T(8,128)S(1)} %get-tuple-element.17), kind=kOutput, calls=%fused_computation.31 | convolution fusion | flops 676855808 | bytes 12861440 | tf_op jit(solution)/shard_map/hqk,khd->qhd/dot_general | solution.py:91
  182.8 1.8 collective-permute-start.6
  184.6 1.3 reduce-window.6
  186.3 10.2 %all-gather.5.cloned.1.call-done = bf16[3200,1024]{1,0:T(8,128)(2,1)} async-done(((bf16[200,1024]{1,0:T(8,128)(2,1)}), bf16[3200,1024]{1,0:T(8,128)(2,1)}) %all-gather.5.cloned.1.call-update) | async-done | bytes 6553616 | tf_op jit(solution)/shard_map/all_gather | solution.py:51
  196.6 5.0 %fusion.17 = bf16[512,1600]{0,1:T(8,128)(2,1)} fusion(bf16[512,1024]{0,1:T(8,128)(2,1)S(1)} %bitcast.59, bf16[3200,1024]{1,0:T(8,128)(2,1)} %all-gather.5.cloned.1.call-done), kind=kOutput, calls=%fused_computation.23 | convolution fusion | flops 1678540800 | bytes 5963776 | tf_op jit(solution)/shard_map/dot_general | solution.py:97
  201.6 6.6 %collective-permute-done.6 = bf16[512,1024]{0,1:T(8,128)(2,1)S(1)} collective-permute-done((bf16[512,1024]{0,1:T(8,128)(2,1)S(1)}, bf16[512,1024]{0,1:T(8,128)(2,1)S(1)}, u32[]{:S(2)}, u32[]{:S(2)}) %collective-permute-start.6) | collective-permute-done | bytes 1048608 | tf_op jit(solution)/shard_map/ppermute | solution.py:20
  208.2 8.5 %convolution_convert_fusion = bf16[1024,1600]{0,1:T(8,128)(2,1)} fusion(s32[512]{0:T(512)S(1)} %multiply_add_fusion, bf16[512,1600]{0,1:T(8,128)(2,1)} %fusion.17, bf16[512,1600]{0,1:T(8,128)(2,1)} %param.8, bf16[512,1024]{0,1:T(8,128)(2,1)S(1)} %collective-permute-done.6, bf16[3200,1024]{1,0:T(8,128)(2,1)} %all-gather.5.cloned.1.call-done, ...), kind=kOutput, calls=%fused_computation.14 | convolution fusion | flops 3364159488 | bytes 10887424 | tf_op jit(solution)/shard_map/dot_general | solution.py:114
  216.7 4.3 %copy.18 = bf16[1024,1600]{1,0:T(8,128)(2,1)S(1)} copy(bf16[1024,1600]{0,1:T(8,128)(2,1)} %convolution_convert_fusion) | data formatting | bytes 6553600 | tf_op jit(solution)/shard_map/convert_element_type | solution.py:114
  221.1 87.3 %all_to_all.5 = bf16[16,64,1600]{2,1,0:T(8,128)(2,1)S(1)} all-to-all(bf16[16,64,1600]{2,1,0:T(8,128)(2,1)S(1)} %bitcast.48), channel_id=1, replica_groups=mesh['group'=16,'tp'=2] {'group'}, dimensions={0} | all-to-all | bytes 6553600 | tf_op jit(solution)/shard_map/all_to_all | solution.py:116
  308.3 1.8 copy.38
  (49 shorter events, 2.3 us)
Async XLA Ops:
  6.5 107.8 %all-gather.3.cloned.1.call-start = ((), (), s32[]{:S(2)}) async-start(), calls=%async_computation.1 | async-start | bytes 20889600 | tf_op jit(solution)/shard_map/all_gather | solution.py:30
  9.0 187.6 %all-gather.5.cloned.1.call-start = ((), (), s32[]{:S(2)}) async-start(), calls=%async_computation.2 | async-start | bytes 6963200 | tf_op jit(solution)/shard_map/all_gather | solution.py:51
  9.0 38.0 %collective-permute-start = (bf16[512,1600]{0,1:T(8,128)(2,1)}, bf16[512,1600]{0,1:T(8,128)(2,1)}, u32[]{:S(2)}, u32[]{:S(2)}) collective-permute-start(bf16[512,1600]{0,1:T(8,128)(2,1)} %param.8), channel_id=1, source_target_pairs={{1,0},{0,1},{3,2},{2,3},{5,4},{4,5},{7,6},{6,7},{9,8},{8,9},{11,10... | collective-permute-start | bytes 4915208 | tf_op jit(solution)/shard_map/ppermute | solution.py:20
  11.3 37.2 %copy-start.8 = (bf16[1024,200]{0,1:T(8,128)(2,1)S(1)}, bf16[1024,200]{0,1:T(8,128)(2,1)}, u32[]{:S(2)}) copy-start(bf16[1024,200]{0,1:T(8,128)(2,1)} %param.12) | copy-start | bytes 1228804
  11.3 38.7 %copy-start.5 = (bf16[1600]{0:T(1024)(128)(2,1)S(1)}, bf16[1600]{0:T(1024)(128)(2,1)}, u32[]{:S(2)}) copy-start(bf16[1600]{0:T(1024)(128)(2,1)} %param.9) | copy-start | bytes 9604
  11.4 69.8 %copy-start.6 = (s32[512]{0:T(512)S(1)}, s32[512]{0:T(512)}, u32[]{:S(2)}) copy-start(s32[512]{0:T(512)} %param.14) | copy-start | bytes 6148
  11.4 72.2 %copy-start.7 = (f32[2,1024]{1,0:T(2,128)S(1)}, f32[2,1024]{1,0:T(2,128)}, u32[]{:S(2)}) copy-start(f32[2,1024]{1,0:T(2,128)} %param.11) | copy-start | bytes 24580
  48.6 1.4 collective-permute-start.5
  50.1 34.4 %collective-permute-start.1 = (bf16[1,1600]{1,0:T(2,128)(2,1)S(1)}, bf16[1,1600]{1,0:T(2,128)(2,1)S(1)}, u32[]{:S(2)}, u32[]{:S(2)}) collective-permute-start(bf16[1,1600]{1,0:T(2,128)(2,1)S(1)} %reshape.96), channel_id=1, source_target_pairs={{1,0},{0,1},{3,2},{2,3},{5,4},{4,5},{7,6},{6,7},{9,8},{8,9},{11,10... | collective-permute-start | bytes 9608 | tf_op jit(solution)/shard_map/ppermute | solution.py:20
  81.3 3.2 collective-permute-start.3
  128.6 2.7 copy-start
  128.8 22.9 %collective-permute-start.2 = (bf16[128,1024]{1,0:T(8,128)(2,1)S(1)}, bf16[128,1024]{1,0:T(8,128)(2,1)}, u32[]{:S(2)}, u32[]{:S(2)}) collective-permute-start(bf16[128,1024]{1,0:T(8,128)(2,1)S(1)} %constant_dynamic-slice_fusion.1), channel_id=1, source_target_pairs={{0,2},{2,0},{4,6},{6,4},{8,10},{10,8},{12,14},{14,12},{16,18},{18,... | collective-permute-start | bytes 786440 | tf_op jit(solution)/shard_map/ppermute | solution.py:15
  150.0 4.2 %collective-permute-start.4 = (bf16[128,1024]{1,0:T(8,128)(2,1)}, bf16[128,1024]{1,0:T(8,128)(2,1)}, u32[]{:S(2)}, u32[]{:S(2)}) collective-permute-start(bf16[128,1024]{1,0:T(8,128)(2,1)} %constant_dynamic-slice_fusion), channel_id=1, source_target_pairs={{0,2},{2,0},{4,6},{6,4},{8,10},{10,8},{12,14},{14,12},{16,18},{18,... | collective-permute-start | bytes 786440 | tf_op jit(solution)/shard_map/ppermute | solution.py:15
  152.8 1.5 copy-start.1
  154.2 6.5 %copy-start.3 = (pred[512,640]{1,0:T(8,128)(4,1)S(1)}, pred[512,640]{1,0:T(8,128)(4,1)}, u32[]{:S(2)}) copy-start(pred[512,640]{1,0:T(8,128)(4,1)} %broadcast_compare_fusion) | copy-start | bytes 983044
  160.8 16.0 %copy-start.2 = (bf16[640,1024]{0,1:T(8,128)(2,1)S(1)}, bf16[640,1024]{0,1:T(8,128)(2,1)}, u32[]{:S(2)}) copy-start(bf16[640,1024]{0,1:T(8,128)(2,1)} %copy.19) | copy-start | bytes 3932164
  176.8 7.8 %copy-start.4 = (s32[512,1]{0,1:T(1,128)S(1)}, s32[512,1]{0,1:T(1,128)}, u32[]{:S(2)}) copy-start(s32[512,1]{0,1:T(1,128)} %param.15) | copy-start | bytes 6148
  182.8 25.4 %collective-permute-start.6 = (bf16[512,1024]{0,1:T(8,128)(2,1)S(1)}, bf16[512,1024]{0,1:T(8,128)(2,1)S(1)}, u32[]{:S(2)}, u32[]{:S(2)}) collective-permute-start(bf16[512,1024]{0,1:T(8,128)(2,1)S(1)} %bitcast.58), channel_id=1, source_target_pairs={{1,0},{0,1},{3,2},{2,3},{5,4},{4,5},{7,6},{6,7},{9,8},{8,9},{11,10... | collective-permute-start | bytes 3145736 | tf_op jit(solution)/shard_map/ppermute | solution.py:20
  186.3 21.9 %copy-start.9 = (f32[1600]{0:T(1024)S(1)}, f32[1600]{0:T(1024)}, u32[]{:S(2)}) copy-start(f32[1600]{0:T(1024)} %param.13) | copy-start | bytes 19204
Sparse Core Ops, SparseCore 0:
  9.1 105.1 all-gather.2
  116.6 79.9 all-gather.4

commit v3 on v2

--- a/solution.py
+++ b/solution.py
@@ -3,6 +3,8 @@
 import jax
 import jax.numpy as jnp
 from jax import lax
+from jax.experimental import pallas as pl
+from jax.experimental.pallas import tpu as pltpu
 from jax.sharding import PartitionSpec as P
 
 HD = 128
@@ -18,6 +20,136 @@
 def from_next(value, axis):
     count = lax.axis_size(axis)
     return lax.ppermute(value, axis, [((i + 1) % count, i) for i in range(count)])
+
+
+def attend_kernel(q_ref, k_ref, v_ref, kp_ref, vp_ref, row_ref, own_ref, pair_ref, out_ref):
+    query = q_ref[...]
+    over = (((1,), (1,)), ((), ()))
+    scale = 1.0 / math.sqrt(HD)
+    near = lax.dot_general(query, k_ref[...], over, preferred_element_type=jnp.float32) * scale
+    far = lax.dot_general(query, kp_ref[...], over, preferred_element_type=jnp.float32) * scale
+    near = jnp.where(row_ref[...] == own_ref[...], near, -jnp.inf)
+    far = jnp.where(row_ref[...] == pair_ref[...], far, -jnp.inf)
+    top = jnp.maximum(
+        jnp.max(near, axis=-1, keepdims=True), jnp.max(far, axis=-1, keepdims=True)
+    )
+    near, far = jnp.exp(near - top), jnp.exp(far - top)
+    share = 1.0 / (jnp.sum(near, axis=-1, keepdims=True) + jnp.sum(far, axis=-1, keepdims=True))
+    near, far = (near * share).astype(jnp.bfloat16), (far * share).astype(jnp.bfloat16)
+    total = jnp.dot(near, v_ref[...], preferred_element_type=jnp.float32)
+    total += jnp.dot(far, vp_ref[...], preferred_element_type=jnp.float32)
+    out_ref[...] = total.astype(jnp.bfloat16)
+
+
+def attend(query, keys, values, paired_keys, paired_values, ids, paired_ids):
+    rows, width = query.shape
+    seam = paired_keys.shape[0]
+    block = pl.BlockSpec((rows, HD), lambda h: (0, h))
+    seam_block = pl.BlockSpec((seam, HD), lambda h: (0, h))
+    fixed = lambda shape: pl.BlockSpec(shape, lambda h: (0, 0))
+    return pl.pallas_call(
+        attend_kernel,
+        grid=(width // HD,),
+        out_shape=jax.ShapeDtypeStruct((rows, width), jnp.bfloat16),
+        in_specs=[
+            block, block, block, seam_block, seam_block,
+            fixed((rows, 1)), fixed((1, rows)), fixed((1, seam)),
+        ],
+        out_specs=block,
+        compiler_params=pltpu.CompilerParams(vmem_limit_bytes=32 * 2**20),
+        cost_estimate=pl.CostEstimate(
+            flops=4 * rows * (rows + seam) * width,
+            transcendentals=rows * (rows + seam) * width // HD,
+            bytes_accessed=8 * rows * width,
+        ),
+    )(
+        query, keys, values, paired_keys, paired_values,
+        ids[:, None], ids[None, :], paired_ids[None, :],
+    )
+
+
+def route_kernel(count, place_ref, mixed_ref, out_ref, outbox, send_sem, recv_sem, keep_sem):
+    me = lax.axis_index("group")
+    capacity = outbox.shape[1]
+    rows = mixed_ref.shape[0]
+    barrier = pltpu.get_barrier_semaphore()
+
+    @pl.loop(1, count)
+    def _(step):
+        pl.semaphore_signal(
+            barrier, inc=1, device_id={"group": lax.rem(me + step, count)},
+            device_id_type=pl.DeviceIdType.MESH,
+        )
+
+    pl.semaphore_wait(barrier, count - 1)
+
+    def pick(owner):
+        slots = lax.broadcasted_iota(jnp.int32, (capacity, rows), 0) + owner * capacity
+        select = (slots == place_ref[...]).astype(jnp.float32).astype(jnp.bfloat16)
+        return jnp.dot(select, mixed_ref[...], preferred_element_type=jnp.float32).astype(
+            jnp.bfloat16
+        )
+
+    def sending(step):
+        ahead = 1 + lax.rem(step - 1 + count // 2 - 1, count - 1)
+        peer = lax.rem(me + ahead, count)
+        return peer, pltpu.make_async_remote_copy(
+            src_ref=outbox.at[step],
+            dst_ref=out_ref.at[me],
+            send_sem=send_sem.at[step],
+            recv_sem=recv_sem.at[me],
+            device_id={"group": peer},
+            device_id_type=pl.DeviceIdType.MESH,
+        )
+
+    @pl.loop(1, count)
+    def _(step):
+        peer, copy = sending(step)
+        outbox[step] = pick(peer)
+        copy.start()
+
+    outbox[0] = pick(me)
+    keep = pltpu.make_async_copy(outbox.at[0], out_ref.at[me], keep_sem)
+    keep.start()
+
+    @pl.loop(1, count)
+    def _(step):
+        source = lax.rem(me + step, count)
+        pltpu.make_async_remote_copy(
+            src_ref=outbox.at[step],
+            dst_ref=out_ref.at[source],
+            send_sem=send_sem.at[step],
+            recv_sem=recv_sem.at[source],
+            device_id={"group": source},
+            device_id_type=pl.DeviceIdType.MESH,
+        ).wait()
+
+    keep.wait()
+
+
+def route(place, mixed, count, capacity):
+    rows, feat = mixed.shape
+    return pl.pallas_call(
+        lambda *refs: route_kernel(count, *refs),
+        name="route",
+        out_shape=jax.ShapeDtypeStruct((count, capacity, feat), jnp.bfloat16),
+        in_specs=[pl.BlockSpec(memory_space=pltpu.VMEM)] * 2,
+        out_specs=pl.BlockSpec(memory_space=pl.ANY),
+        scratch_shapes=[
+            pltpu.VMEM((count, capacity, feat), jnp.bfloat16),
+            pltpu.SemaphoreType.DMA((count,)),
+            pltpu.SemaphoreType.DMA((count,)),
+            pltpu.SemaphoreType.DMA,
+        ],
+        compiler_params=pltpu.CompilerParams(
+            collective_id=0, has_side_effects=True, vmem_limit_bytes=32 * 2**20
+        ),
+        cost_estimate=pl.CostEstimate(
+            flops=2 * count * capacity * rows * feat,
+            transcendentals=0,
+            bytes_accessed=4 * count * capacity * feat,
+        ),
+    )(place[None, :], mixed)
 
 
 def shards(tokens, norm_gain, w_qkv, qk_gain, w_out, layer_scale, request, owner):
@@ -71,25 +203,10 @@
     seam = jnp.where(parity == 0, rows - SHARE, 0).astype(jnp.int32)
     key_window = lax.dynamic_slice_in_dim(knorm, seam, SHARE, 0)
     id_window = lax.dynamic_slice_in_dim(request, seam, SHARE, 0)
-    paired_key, paired_ids = swapped((key_window, id_window), "group", 0)
-    all_keys = jnp.concatenate([knorm, paired_key], axis=0)
-    all_ids = jnp.concatenate([request, paired_ids], axis=0)
-    qheads = qnorm.reshape(rows, head_count, HD)
-    kheads = all_keys.reshape(rows + SHARE, head_count, HD)
-    scores = jnp.einsum(
-        "qhd,khd->hqk", qheads, kheads, preferred_element_type=jnp.float32
-    ) / math.sqrt(HD)
-    same = request[:, None] == all_ids[None, :]
-    scores = jnp.where(same[None], scores, -jnp.inf)
-    top = jnp.max(scores, axis=-1, keepdims=True)
-    expo = jnp.exp(scores - top)
-    probs = (expo / jnp.sum(expo, axis=-1, keepdims=True)).astype(jnp.bfloat16)
-
+    paired_keys, paired_ids = swapped((key_window, id_window), "group", 0)
     value_window = lax.dynamic_slice_in_dim(value, seam, SHARE, 0)
-    all_values = jnp.concatenate([value, swapped(value_window, "group", 0)], axis=0)
-    vheads = all_values.reshape(rows + SHARE, head_count, HD)
-    attended = jnp.einsum("hqk,khd->qhd", probs, vheads, preferred_element_type=jnp.float32)
-    attended = attended.astype(jnp.bfloat16).reshape(rows, local_width)
+    paired_values = swapped(value_window, "group", 0)
+    attended = attend(qnorm, knorm, value, paired_keys, paired_values, request, paired_ids)
 
     branch = jnp.zeros((rows, feat_local), jnp.float32)
     for step in range(tp_count):
@@ -108,12 +225,7 @@
     )
     slot = jnp.sum((jnp.cumsum(onehot, axis=0) - onehot) * onehot, axis=-1)
     place = target * capacity + slot
-    select = (
-        jnp.arange(group_count * capacity, dtype=jnp.int32)[:, None] == place[None, :]
-    ).astype(jnp.bfloat16)
-    outbox = jnp.dot(select, mixed, preferred_element_type=jnp.float32).astype(jnp.bfloat16)
-    outbox = outbox.reshape(group_count, capacity, feat_local)
-    inbox = lax.all_to_all(outbox, "group", split_axis=0, concat_axis=0, tiled=True)
+    inbox = route(place, mixed, group_count, capacity)
     return inbox[None]
 
 

time: 317 us -> 292 us (0.921)
  Pallas kernels: 0 us -> 88.8 us
  blocking collectives: 102 us -> 14.4 us
  other arithmetic: 24.4 us -> 5.15 us
  matrix products: 40.3 us -> 22.4 us
  waiting for transfers between devices: 80.1 us -> 94.4 us
    pallas_call x0 -> x2, Pallas kernels: none -> 88.8 us  [the longest x1 78.3 us: route(): pl.pallas_call(lambda *refs: route_kernel(count, *refs), name='route', ou...]
    all_to_all x1 -> x0, blocking collectives: 87.3 us -> none  [shards(): lax.all_to_all(outbox, 'group', split_axis=0, concat_axis=0, tiled=True)]
    dot_general x3 -> x0, matrix products: 21 us -> none  [the longest x1 8.52 us: shards(): jnp.dot(select, mixed, preferred_element_type=jnp.float32)]
    all_gather x1, waiting for transfers between devices: 10.2 us -> 27.6 us  [shards(): w_o = lax.all_gather(w_piece, 'group', axis=0, tiled=True)]
    sub x1 -> x0, other arithmetic: 16 us -> none  [shards(): expo = jnp.exp(scores - top)]
    ppermute x3, waiting for transfers between devices: 40.6 us -> 35 us  [from_next(): lax.ppermute(value, axis, [((i + 1) % count, i) for i in range(count)])]
    unnamed x1 -> x0, other arithmetic: 3.68 us -> none
    dot_general x1 -> x2, matrix products: 4.99 us -> 8.06 us  [shards(): lax.dot_general(attended, w_o[step], (((1,), (1,)), ((), ())), preferred_...]
  transfers between devices with their start and end apart: 9 -> 9, of which waited for: 5 -> 6; matrix products, arithmetic and copies ran while one was open for 20% -> 11% of each run, Pallas kernels for 0% -> 4%
where the time goes in v3:
time: 292 us
  waiting for transfers between devices  94.4 us (32%)
  Pallas kernels  88.8 us (30%)
  starting transfers between devices  37.7 us (13%)
  matrix products  22.4 us (8%)
  local copies, waits for them, and re-layouts  15.5 us (5%)
  blocking collectives  14.4 us (5%)
  between operations  13.6 us (5%)
  other arithmetic  5.15 us (2%)
    pallas_call x1, Pallas kernels, route(): pl.pallas_call(lambda *refs: route_kernel(count, *refs), name='route', ou...  78.3 us
    ppermute x3, waiting for transfers between devices, from_next(): lax.ppermute(value, axis, [((i + 1) % count, i) for i in range(count)])  35 us
    ppermute x3, starting transfers between devices, from_next(): lax.ppermute(value, axis, [((i + 1) % count, i) for i in range(count)])  35 us
    all_gather x1, waiting for transfers between devices, shards(): lax.all_gather(w_qkv.reshape(w_qkv.shape[0], 3 * local_width), 'group', a...  30.6 us
    all_gather x1, waiting for transfers between devices, shards(): w_o = lax.all_gather(w_piece, 'group', axis=0, tiled=True)  27.6 us
    psum x1, blocking collectives, shards(): lax.psum((jnp.sum(query * query, axis=-1), jnp.sum(key_rows * key_rows, a...  14.4 us
    dot_general x1, matrix products, shards(): qkv = jnp.dot(normed, w_all, preferred_element_type=jnp.float32)  14.3 us
    pallas_call x1, Pallas kernels, attend(): pl.pallas_call(attend_kernel, grid=(width // HD,), out_shape=jax.ShapeDty...  10.5 us
  transfers between devices with their start and end apart: 9, of which 6 were waited for; matrix products, arithmetic and copies ran while one was open for 11% of the time, Pallas kernels for 4%

profile of v3, /device:TPU:1, one launch (start us, length us, event | category | flops | bytes accessed | tf_op | source)
XLA Modules:
  0.0 291.9 jit_solution(14993253191169475077)
XLA Ops:
  6.5 2.4 copy.27
  9.0 2.1 collective-permute-start
  11.4 1.6 constant_dynamic-update-slice_fusion.1
  13.0 34.0 %collective-permute-done = bf16[512,1600]{0,1:T(8,128)(2,1)} collective-permute-done((bf16[512,1600]{0,1:T(8,128)(2,1)}, bf16[512,1600]{0,1:T(8,128)(2,1)}, u32[]{:S(2)}, u32[]{:S(2)}) %collective-permute-start) | collective-permute-done | bytes 1638432 | tf_op jit(solution)/shard_map/ppermute | solution.py:22
  47.0 1.6 constant_dynamic-update-slice_fusion
  48.6 1.4 collective-permute-start.5
  50.1 31.1 %collective-permute-start.1 = (bf16[1,1600]{1,0:T(2,128)(2,1)S(1)}, bf16[1,1600]{1,0:T(2,128)(2,1)S(1)}, u32[]{:S(2)}, u32[]{:S(2)}) collective-permute-start(bf16[1,1600]{1,0:T(2,128)(2,1)S(1)} %reshape.63), channel_id=1, source_target_pairs={{1,0},{0,1},{3,2},{2,3},{5,4},{4,5},{7,6},{6,7},{9,8},{8,9},{11,10... | collective-permute-start | bytes 9608 | tf_op jit(solution)/shard_map/ppermute | solution.py:22
  81.2 0.3 dynamic_update_slice.16
  81.5 1.1 collective-permute-done.1
  82.7 0.3 dynamic_update_slice.17
  82.9 0.8 fusion
  83.7 30.6 %all-gather.3.cloned.1.call-done = bf16[3200,3072]{1,0:T(8,128)(2,1)} async-done(((bf16[200,3072]{1,0:T(8,128)(2,1)}), bf16[3200,3072]{1,0:T(8,128)(2,1)}) %all-gather.3.cloned.1.call-update) | async-done | bytes 19660816 | tf_op jit(solution)/shard_map/all_gather | solution.py:162
  114.3 14.3 %fusion.3 = f32[512,3072]{1,0:T(8,128)S(1)} fusion(bf16[3200,3072]{1,0:T(8,128)(2,1)} %all-gather.3.cloned.1.call-done, bf16[512,3200]{0,1:T(8,128)(2,1)S(1)} %constant_dynamic-update-slice_fusion, f32[3200]{0:T(1024)S(1)} %mul.113, f32[512]{0:T(512)S(1)} %add_rsqrt_fusion.2), kind=kOutput, calls=%fused_computation.6 | convolution fusion | flops 10072883200 | bytes 29243904 | tf_op jit(solution)/shard_map/dot_general | solution.py:188
  128.8 2.5 copy-done.1
  131.3 0.3 multiply_reduce_fusion
  131.6 14.4 %all-reduce = (f32[512]{0:T(512)S(1)}, f32[512]{0:T(512)S(1)}) all-reduce(f32[512]{0:T(512)S(1)} %get-tuple-element.10, f32[512]{0:T(512)S(1)} %get-tuple-element.9), channel_id=1, replica_groups=mesh['group'=16,'tp'=2] {'tp'}, use_global_device_ids=true, to_apply=%region_5.6 | all-reduce | flops 1024 | bytes 8192 | tf_op jit(solution)/shard_map/psum | solution.py:192
  146.0 2.7 multiply_convert_fusion
  148.7 0.7 constant_dynamic-slice_fusion.1
  149.4 0.7 collective-permute-start.2
  150.2 0.7 constant_dynamic-slice_fusion
  151.0 0.5 collective-permute-start.4
  151.6 0.8 collective-permute-done.4
  152.4 0.4 collective-permute-done.3.vp_ref
  152.8 10.5 %shard_map.82 = bf16[512,1024]{1,0:T(8,128)(2,1)} custom-call(bf16[512,1024]{1,0:T(8,128)(2,1)S(1)} %get-tuple-element.14.q_ref, bf16[512,1024]{1,0:T(8,128)(2,1)S(1)} %get-tuple-element.13.k_ref, bf16[512,1024]{1,0:T(8,128)(2,1)S(1)} %slice.61.v_ref, bf16[128,1024]{1,0:T(8,128)(2,1)} %collective-permute-done.2.kp_ref, ...), custom_call_target="tpu_custom_call" | custom-call | flops 1342177280 | bytes 4194304 | tf_op jit(solution)/shard_map/pallas_call | solution.py:50
  163.3 1.8 collective-permute-start.6
  165.0 2.7 copy.23
  167.8 1.2 reduce-window.6
  169.3 27.6 %all-gather.5.cloned.1.call-done = bf16[3200,1024]{1,0:T(8,128)(2,1)} async-done(((bf16[200,1024]{1,0:T(8,128)(2,1)}), bf16[3200,1024]{1,0:T(8,128)(2,1)}) %all-gather.5.cloned.1.call-update) | async-done | bytes 6553616 | tf_op jit(solution)/shard_map/all_gather | solution.py:183
  196.9 4.5 %fusion.11 = bf16[512,1600]{1,0:T(8,128)(2,1)S(1)} fusion(bf16[512,1024]{1,0:T(8,128)(2,1)} %shard_map.82, bf16[3200,1024]{1,0:T(8,128)(2,1)} %all-gather.5.cloned.1.call-done), kind=kOutput, calls=%fused_computation.13 | convolution fusion | flops 1678540800 | bytes 5963776 | tf_op jit(solution)/shard_map/dot_general | solution.py:214
  201.4 3.6 %add_convert_fusion.refs_1_ = bf16[512,1600]{1,0:T(8,128)(2,1)S(1)} fusion(f32[512,1600]{1,0:T(8,128)S(1)} %copy.23, bf16[512,1600]{1,0:T(8,128)(2,1)S(1)} %fusion.11, bf16[512,1024]{1,0:T(8,128)(2,1)} %collective-permute-done.6, bf16[3200,1024]{1,0:T(8,128)(2,1)S(1)} %copy-done.5, f32[1600]{0:T(1024)S(1)} %copy-done.7), kind=kOutput, calls=%fused_computation.5 | convolution fusion | flops 1683456000 | bytes 11083776 | tf_op jit(solution)/shard_map/dot_general | solution.py:214
  205.0 78.3 %route.1 = bf16[16,64,1600]{2,1,0:T(8,128)(2,1)S(1)} custom-call(s32[1,512]{1,0:T(1,128)S(1)} %bitcast_add_fusion.refs_0_, bf16[512,1600]{1,0:T(8,128)(2,1)S(1)} %add_convert_fusion.refs_1_), custom_call_target="tpu_custom_call" | custom-call | flops 1677721600 | bytes 6553600 | tf_op jit(solution)/shard_map/route/pallas_call | solution.py:132
  283.3 1.8 copy.34
  (40 shorter events, 1.2 us)
Async XLA Ops:
  6.5 107.8 %all-gather.3.cloned.1.call-start = ((), (), s32[]{:S(2)}) async-start(), calls=%async_computation | async-start | bytes 20889600 | tf_op jit(solution)/shard_map/all_gather | solution.py:162
  9.0 187.9 %all-gather.5.cloned.1.call-start = ((), (), s32[]{:S(2)}) async-start(), calls=%async_computation.1 | async-start | bytes 6963200 | tf_op jit(solution)/shard_map/all_gather | solution.py:183
  9.0 38.0 %collective-permute-start = (bf16[512,1600]{0,1:T(8,128)(2,1)}, bf16[512,1600]{0,1:T(8,128)(2,1)}, u32[]{:S(2)}, u32[]{:S(2)}) collective-permute-start(bf16[512,1600]{0,1:T(8,128)(2,1)} %param.8), channel_id=1, source_target_pairs={{1,0},{0,1},{3,2},{2,3},{5,4},{4,5},{7,6},{6,7},{9,8},{8,9},{11,10... | collective-permute-start | bytes 4915208 | tf_op jit(solution)/shard_map/ppermute | solution.py:22
  11.3 37.2 %copy-start.6 = (bf16[1024,200]{0,1:T(8,128)(2,1)S(1)}, bf16[1024,200]{0,1:T(8,128)(2,1)}, u32[]{:S(2)}) copy-start(bf16[1024,200]{0,1:T(8,128)(2,1)} %param.12) | copy-start | bytes 1228804
  11.3 38.7 %copy-start.3 = (bf16[1600]{0:T(1024)(128)(2,1)S(1)}, bf16[1600]{0:T(1024)(128)(2,1)}, u32[]{:S(2)}) copy-start(bf16[1600]{0:T(1024)(128)(2,1)} %param.9) | copy-start | bytes 9604
  11.4 69.8 %copy-start.4 = (f32[2,1024]{1,0:T(2,128)S(1)}, f32[2,1024]{1,0:T(2,128)}, u32[]{:S(2)}) copy-start(f32[2,1024]{1,0:T(2,128)} %param.11) | copy-start | bytes 24580
  48.6 1.4 collective-permute-start.5
  50.1 32.6 %collective-permute-start.1 = (bf16[1,1600]{1,0:T(2,128)(2,1)S(1)}, bf16[1,1600]{1,0:T(2,128)(2,1)S(1)}, u32[]{:S(2)}, u32[]{:S(2)}) collective-permute-start(bf16[1,1600]{1,0:T(2,128)(2,1)S(1)} %reshape.63), channel_id=1, source_target_pairs={{1,0},{0,1},{3,2},{2,3},{5,4},{4,5},{7,6},{6,7},{9,8},{8,9},{11,10... | collective-permute-start | bytes 9608 | tf_op jit(solution)/shard_map/ppermute | solution.py:22
  128.6 2.7 copy-start.1
  146.0 4.9 %copy-start = (s32[512]{0:T(512)S(1)}, s32[512]{0:T(512)}, u32[]{:S(2)}) copy-start(s32[512]{0:T(512)} %param.14) | copy-start | bytes 6148
  148.7 16.3 %copy-start.2 = (s32[512,1]{0,1:T(1,128)S(1)}, s32[512,1]{0,1:T(1,128)}, u32[]{:S(2)}) copy-start(s32[512,1]{0,1:T(1,128)} %param.15) | copy-start | bytes 6148
  149.4 2.9 %collective-permute-start.2 = (bf16[128,1024]{1,0:T(8,128)(2,1)}, bf16[128,1024]{1,0:T(8,128)(2,1)}, u32[]{:S(2)}, u32[]{:S(2)}) collective-permute-start(bf16[128,1024]{1,0:T(8,128)(2,1)} %constant_dynamic-slice_fusion.1), channel_id=1, source_target_pairs={{0,2},{2,0},{4,6},{6,4},{8,10},{10,8},{12,14},{14,12},{16,18},{18,... | collective-permute-start | bytes 786440 | tf_op jit(solution)/shard_map/ppermute | solution.py:17
  150.9 1.9 collective-permute-start.3
  151.0 1.4 collective-permute-start.4
  163.3 38.1 %collective-permute-start.6 = (bf16[512,1024]{1,0:T(8,128)(2,1)}, bf16[512,1024]{1,0:T(8,128)(2,1)}, u32[]{:S(2)}, u32[]{:S(2)}) collective-permute-start(bf16[512,1024]{1,0:T(8,128)(2,1)} %shard_map.82), channel_id=1, source_target_pairs={{1,0},{0,1},{3,2},{2,3},{5,4},{4,5},{7,6},{6,7},{9,8},{8,9},{11,10... | collective-permute-start | bytes 3145736 | tf_op jit(solution)/shard_map/ppermute | solution.py:22
  169.3 32.1 %copy-start.7 = (f32[1600]{0:T(1024)S(1)}, f32[1600]{0:T(1024)}, u32[]{:S(2)}) copy-start(f32[1600]{0:T(1024)} %param.13) | copy-start | bytes 19204
  196.9 4.5 %copy-start.5 = (bf16[3200,1024]{1,0:T(8,128)(2,1)S(1)}, bf16[3200,1024]{1,0:T(8,128)(2,1)}, u32[]{:S(2)}) copy-start(bf16[3200,1024]{1,0:T(8,128)(2,1)} %all-gather.5.cloned.1.call-done) | copy-start | bytes 19660804
Sparse Core Ops, SparseCore 0:
  9.1 105.1 all-gather.2
  116.6 80.2 all-gather.4

commit v4 on v3

--- a/solution.py
+++ b/solution.py
@@ -177,7 +177,7 @@
     for g in range(group_count):
         for b in range(tp_count):
             t, j = g // per, g % per
-            to_g = ((b - t) % tp_count) * per + j
+            to_g = b * per + j
             pairs.append((g * tp_count + b, to_g * tp_count + t))
     w_piece = lax.ppermute(late_out.T, ("group", "tp"), pairs)
     w_o = lax.all_gather(w_piece, "group", axis=0, tiled=True)
@@ -212,7 +212,10 @@
     for step in range(tp_count):
         onward = from_next(attended, "tp") if step < tp_count - 1 else None
         part = lax.dot_general(
-            attended, w_o[step], (((1,), (1,)), ((), ())), preferred_element_type=jnp.float32
+            attended,
+            lax.dynamic_index_in_dim(w_o, (me_tp + step) % tp_count, 0, keepdims=False),
+            (((1,), (1,)), ((), ())),
+            preferred_element_type=jnp.float32,
         )
         branch = branch + part.astype(jnp.bfloat16).astype(jnp.float32)
         attended = onward

time: 292 us -> 291 us (level)
  blocking collectives: 14.4 us -> 4.37 us
  waiting for transfers between devices: 94.4 us -> 104 us
    psum x1, blocking collectives: 14.4 us -> 4.37 us  [shards(): lax.psum((jnp.sum(query * query, axis=-1), jnp.sum(key_rows * key_rows, a...]
    all_gather x1, waiting for transfers between devices: 30.6 us -> 40.4 us  [shards(): lax.all_gather(w_qkv.reshape(w_qkv.shape[0], 3 * local_width), 'group', a...]
  transfers between devices with their start and end apart: 9 -> 9, of which waited for: 6 -> 4; matrix products, arithmetic and copies ran while one was open for 11% -> 12% of each run, Pallas kernels for 4% -> 4%
where the time goes in v4:
time: 291 us
  waiting for transfers between devices  104 us (36%)
  Pallas kernels  88.8 us (31%)
  starting transfers between devices  37.1 us (13%)
  matrix products  21.2 us (7%)
  local copies, waits for them, and re-layouts  17.1 us (6%)
  between operations  13.6 us (5%)
  other arithmetic  5.13 us (2%)
  blocking collectives  4.37 us (2%)
    pallas_call x1, Pallas kernels, route(): pl.pallas_call(lambda *refs: route_kernel(count, *refs), name='route', ou...  78.3 us
    all_gather x1, waiting for transfers between devices, shards(): lax.all_gather(w_qkv.reshape(w_qkv.shape[0], 3 * local_width), 'group', a...  40.4 us
    ppermute x3, waiting for transfers between devices, from_next(): lax.ppermute(value, axis, [((i + 1) % count, i) for i in range(count)])  34.6 us
    ppermute x3, starting transfers between devices, from_next(): lax.ppermute(value, axis, [((i + 1) % count, i) for i in range(count)])  34.2 us
    all_gather x1, waiting for transfers between devices, shards(): w_o = lax.all_gather(w_piece, 'group', axis=0, tiled=True)  28.6 us
    dot_general x1, matrix products, shards(): qkv = jnp.dot(normed, w_all, preferred_element_type=jnp.float32)  14.4 us
    pallas_call x1, Pallas kernels, attend(): pl.pallas_call(attend_kernel, grid=(width // HD,), out_shape=jax.ShapeDty...  10.5 us
    dot_general x2, matrix products, shards(): lax.dot_general(attended, lax.dynamic_index_in_dim(w_o, (me_tp + step) %...  6.78 us
  transfers between devices with their start and end apart: 9, of which 4 were waited for; matrix products, arithmetic and copies ran while one was open for 12% of the time, Pallas kernels for 4%

profile of v4, /device:TPU:1, one launch (start us, length us, event | category | flops | bytes accessed | tf_op | source)
XLA Modules:
  0.0 291.0 jit_solution(13431385033435072151)
XLA Ops:
  6.5 2.4 copy.27
  9.0 2.1 collective-permute-start
  11.1 0.2 broadcast_in_dim.10
  11.4 1.6 constant_dynamic-update-slice_fusion.1
  13.0 34.0 %collective-permute-done = bf16[512,1600]{0,1:T(8,128)(2,1)} collective-permute-done((bf16[512,1600]{0,1:T(8,128)(2,1)}, bf16[512,1600]{0,1:T(8,128)(2,1)}, u32[]{:S(2)}, u32[]{:S(2)}) %collective-permute-start) | collective-permute-done | bytes 1638432 | tf_op jit(solution)/shard_map/ppermute | solution.py:22
  47.0 1.6 constant_dynamic-update-slice_fusion
  48.6 1.4 collective-permute-start.5
  50.1 32.0 %collective-permute-start.1 = (bf16[1,1600]{1,0:T(2,128)(2,1)S(1)}, bf16[1,1600]{1,0:T(2,128)(2,1)S(1)}, u32[]{:S(2)}, u32[]{:S(2)}) collective-permute-start(bf16[1,1600]{1,0:T(2,128)(2,1)S(1)} %reshape.61), channel_id=1, source_target_pairs={{1,0},{0,1},{3,2},{2,3},{5,4},{4,5},{7,6},{6,7},{9,8},{8,9},{11,10... | collective-permute-start | bytes 9608 | tf_op jit(solution)/shard_map/ppermute | solution.py:22
  82.1 0.3 dynamic_update_slice.16
  82.4 0.7 collective-permute-done.1
  83.2 0.3 dynamic_update_slice.17
  83.4 0.8 fusion
  84.2 40.4 %all-gather.3.cloned.1.call-done = bf16[3200,3072]{1,0:T(8,128)(2,1)} async-done(((bf16[200,3072]{1,0:T(8,128)(2,1)}), bf16[3200,3072]{1,0:T(8,128)(2,1)}) %all-gather.3.cloned.1.call-update) | async-done | bytes 19660816 | tf_op jit(solution)/shard_map/all_gather | solution.py:162
  124.6 14.4 %fusion.3 = f32[512,3072]{1,0:T(8,128)S(1)} fusion(bf16[3200,3072]{1,0:T(8,128)(2,1)} %all-gather.3.cloned.1.call-done, bf16[512,3200]{0,1:T(8,128)(2,1)S(1)} %constant_dynamic-update-slice_fusion, f32[3200]{0:T(1024)S(1)} %mul.113, f32[512]{0:T(512)S(1)} %add_rsqrt_fusion.2), kind=kOutput, calls=%fused_computation.6 | convolution fusion | flops 10072883200 | bytes 29243904 | tf_op jit(solution)/shard_map/dot_general | solution.py:188
  139.1 2.5 copy-done.1
  141.6 0.3 multiply_reduce_fusion
  142.0 4.4 %all-reduce = (f32[512]{0:T(512)S(1)}, f32[512]{0:T(512)S(1)}) all-reduce(f32[512]{0:T(512)S(1)} %get-tuple-element.10, f32[512]{0:T(512)S(1)} %get-tuple-element.9), channel_id=1, replica_groups=mesh['group'=16,'tp'=2] {'tp'}, use_global_device_ids=true, to_apply=%region_5.6 | all-reduce | flops 1024 | bytes 8192 | tf_op jit(solution)/shard_map/psum | solution.py:192
  146.4 2.7 multiply_convert_fusion
  149.0 0.7 constant_dynamic-slice_fusion.1
  149.8 1.0 collective-permute-start.2
  150.8 0.7 constant_dynamic-slice_fusion
  151.6 0.5 collective-permute-start.4
  152.1 3.7 %copy.23 = f32[512,1600]{1,0:T(8,128)} copy(bf16[512,1600]{0,1:T(8,128)(2,1)} %param.8) | data formatting | bytes 4915200 | tf_op jit(solution)/shard_map/convert_element_type | solution.py:222
  155.9 10.5 %shard_map.82 = bf16[512,1024]{1,0:T(8,128)(2,1)} custom-call(bf16[512,1024]{1,0:T(8,128)(2,1)S(1)} %get-tuple-element.14.q_ref, bf16[512,1024]{1,0:T(8,128)(2,1)S(1)} %get-tuple-element.13.k_ref, bf16[512,1024]{1,0:T(8,128)(2,1)S(1)} %slice.39.v_ref, bf16[128,1024]{1,0:T(8,128)(2,1)} %collective-permute-done.2.kp_ref, ...), custom_call_target="tpu_custom_call" | custom-call | flops 1342177280 | bytes 4194304 | tf_op jit(solution)/shard_map/pallas_call | solution.py:50
  166.4 1.2 reduce-window.6
  167.6 0.2 slice_reduce_fusion
  168.0 28.6 %all-gather.5.cloned.1.call-done = bf16[3200,1024]{1,0:T(8,128)(2,1)} async-done(((bf16[200,1024]{1,0:T(8,128)(2,1)}), bf16[3200,1024]{1,0:T(8,128)(2,1)}) %all-gather.5.cloned.1.call-update) | async-done | bytes 6553616 | tf_op jit(solution)/shard_map/all_gather | solution.py:183
  196.6 4.5 %fusion.13 = bf16[512,1600]{1,0:T(8,128)(2,1)S(1)} fusion(bf16[512,1024]{1,0:T(8,128)(2,1)} %shard_map.82, bf16[2,1600,1024]{2,1,0:T(8,128)(2,1)} %bitcast.60, s32[]{:T(128)S(6)} %select_n.47), kind=kOutput, calls=%fused_computation.15 | convolution fusion | flops 1678540800 | bytes 5963780 | tf_op jit(solution)/shard_map/dot_general | solution.py:214
  201.1 0.7 copy-done.6
  201.8 2.3 add_convert_fusion.refs_1_
  204.1 78.3 %route.1 = bf16[16,64,1600]{2,1,0:T(8,128)(2,1)S(1)} custom-call(s32[1,512]{1,0:T(1,128)S(1)} %bitcast_add_fusion.refs_0_, bf16[512,1600]{1,0:T(8,128)(2,1)S(1)} %add_convert_fusion.refs_1_), custom_call_target="tpu_custom_call" | custom-call | flops 1677721600 | bytes 6553600 | tf_op jit(solution)/shard_map/route/pallas_call | solution.py:132
  282.4 1.8 copy.34
  (42 shorter events, 0.7 us)
Async XLA Ops:
  6.5 118.0 %all-gather.3.cloned.1.call-start = ((), (), s32[]{:S(2)}) async-start(), calls=%async_computation | async-start | bytes 20889600 | tf_op jit(solution)/shard_map/all_gather | solution.py:162
  9.0 187.6 %all-gather.5.cloned.1.call-start = ((), (), s32[]{:S(2)}) async-start(), calls=%async_computation.1 | async-start | bytes 6963200 | tf_op jit(solution)/shard_map/all_gather | solution.py:183
  9.0 38.0 %collective-permute-start = (bf16[512,1600]{0,1:T(8,128)(2,1)}, bf16[512,1600]{0,1:T(8,128)(2,1)}, u32[]{:S(2)}, u32[]{:S(2)}) collective-permute-start(bf16[512,1600]{0,1:T(8,128)(2,1)} %param.8), channel_id=1, source_target_pairs={{1,0},{0,1},{3,2},{2,3},{5,4},{4,5},{7,6},{6,7},{9,8},{8,9},{11,10... | collective-permute-start | bytes 4915208 | tf_op jit(solution)/shard_map/ppermute | solution.py:22
  11.3 37.2 %copy-start.7 = (bf16[1024,200]{0,1:T(8,128)(2,1)S(1)}, bf16[1024,200]{0,1:T(8,128)(2,1)}, u32[]{:S(2)}) copy-start(bf16[1024,200]{0,1:T(8,128)(2,1)} %param.12) | copy-start | bytes 1228804
  11.3 38.7 %copy-start.4 = (bf16[1600]{0:T(1024)(128)(2,1)S(1)}, bf16[1600]{0:T(1024)(128)(2,1)}, u32[]{:S(2)}) copy-start(bf16[1600]{0:T(1024)(128)(2,1)} %param.9) | copy-start | bytes 9604
  11.4 70.7 %copy-start.5 = (f32[2,1024]{1,0:T(2,128)S(1)}, f32[2,1024]{1,0:T(2,128)}, u32[]{:S(2)}) copy-start(f32[2,1024]{1,0:T(2,128)} %param.11) | copy-start | bytes 24580
  48.6 1.4 collective-permute-start.5
  50.1 33.1 %collective-permute-start.1 = (bf16[1,1600]{1,0:T(2,128)(2,1)S(1)}, bf16[1,1600]{1,0:T(2,128)(2,1)S(1)}, u32[]{:S(2)}, u32[]{:S(2)}) collective-permute-start(bf16[1,1600]{1,0:T(2,128)(2,1)S(1)} %reshape.61), channel_id=1, source_target_pairs={{1,0},{0,1},{3,2},{2,3},{5,4},{4,5},{7,6},{6,7},{9,8},{8,9},{11,10... | collective-permute-start | bytes 9608 | tf_op jit(solution)/shard_map/ppermute | solution.py:22
  139.0 2.7 copy-start.1
  146.3 5.1 %copy-start = (s32[512]{0:T(512)S(1)}, s32[512]{0:T(512)}, u32[]{:S(2)}) copy-start(s32[512]{0:T(512)} %param.14) | copy-start | bytes 6148
  149.8 6.1 %collective-permute-start.2 = (bf16[128,1024]{1,0:T(8,128)(2,1)}, bf16[128,1024]{1,0:T(8,128)(2,1)}, u32[]{:S(2)}, u32[]{:S(2)}) collective-permute-start(bf16[128,1024]{1,0:T(8,128)(2,1)} %constant_dynamic-slice_fusion.1), channel_id=1, source_target_pairs={{0,2},{2,0},{4,6},{6,4},{8,10},{10,8},{12,14},{14,12},{16,18},{18,... | collective-permute-start | bytes 786440 | tf_op jit(solution)/shard_map/ppermute | solution.py:17
  151.5 4.4 %collective-permute-start.3 = (bf16[128,1024]{1,0:T(8,128)(2,1)}, bf16[128,1024]{1,0:T(8,128)(2,1)}, u32[]{:S(2)}, u32[]{:S(2)}) collective-permute-start(bf16[128,1024]{1,0:T(8,128)(2,1)} %constant_dynamic-slice_fusion), channel_id=1, source_target_pairs={{0,2},{2,0},{4,6},{6,4},{8,10},{10,8},{12,14},{14,12},{16,18},{18,... | collective-permute-start | bytes 786440 | tf_op jit(solution)/shard_map/ppermute | solution.py:17
  151.6 4.3 %collective-permute-start.4 = (s32[128]{0:T(128)S(1)}, s32[128]{0:T(128)S(1)}, u32[]{:S(2)}, u32[]{:S(2)}) collective-permute-start(s32[128]{0:T(128)S(1)} %dynamic_slice.18), channel_id=1, source_target_pairs={{0,2},{2,0},{4,6},{6,4},{8,10},{10,8},{12,14},{14,12},{16,18},{18,... | collective-permute-start | bytes 1544 | tf_op jit(solution)/shard_map/ppermute | solution.py:17
  155.7 10.7 %copy-start.3 = (s32[512,1]{0,1:T(1,128)S(1)}, s32[512,1]{0,1:T(1,128)}, u32[]{:S(2)}) copy-start(s32[512,1]{0,1:T(1,128)} %param.15) | copy-start | bytes 6148
  166.4 34.7 %collective-permute-start.6 = (bf16[512,1024]{1,0:T(8,128)(2,1)}, bf16[512,1024]{1,0:T(8,128)(2,1)S(1)}, u32[]{:S(2)}, u32[]{:S(2)}) collective-permute-start(bf16[512,1024]{1,0:T(8,128)(2,1)} %shard_map.82), channel_id=1, source_target_pairs={{1,0},{0,1},{3,2},{2,3},{5,4},{4,5},{7,6},{6,7},{9,8},{8,9},{11,10... | collective-permute-start | bytes 3145736 | tf_op jit(solution)/shard_map/ppermute | solution.py:22
  196.6 4.5 %copy-start.2 = (f32[512,1600]{1,0:T(8,128)S(1)}, f32[512,1600]{1,0:T(8,128)}, u32[]{:S(2)}) copy-start(f32[512,1600]{1,0:T(8,128)} %copy.23) | copy-start | bytes 9830404
  196.6 5.2 %copy-start.6 = (bf16[3200,1024]{1,0:T(8,128)(2,1)S(1)}, bf16[3200,1024]{1,0:T(8,128)(2,1)}, u32[]{:S(2)}) copy-start(bf16[3200,1024]{1,0:T(8,128)(2,1)} %all-gather.5.cloned.1.call-done) | copy-start | bytes 19660804
  196.6 5.2 %copy-start.8 = (f32[1600]{0:T(1024)S(1)}, f32[1600]{0:T(1024)}, u32[]{:S(2)}) copy-start(f32[1600]{0:T(1024)} %param.13) | copy-start | bytes 19204
Sparse Core Ops, SparseCore 0:
  9.1 115.4 all-gather.2
  126.9 69.6 all-gather.4

commit v5 on v4

--- a/solution.py
+++ b/solution.py
@@ -68,6 +68,15 @@
     )
 
 
+def flipped(index, mask, count):
+    if count & (count - 1):
+        return lax.rem(index + mask, count)
+    bits = range(count.bit_length() - 1)
+    return sum(
+        lax.rem(lax.div(index, 2**bit) + lax.div(mask, 2**bit), 2) * 2**bit for bit in bits
+    )
+
+
 def route_kernel(count, place_ref, mixed_ref, out_ref, outbox, send_sem, recv_sem, keep_sem):
     me = lax.axis_index("group")
     capacity = outbox.shape[1]
@@ -91,8 +100,7 @@
         )
 
     def sending(step):
-        ahead = 1 + lax.rem(step - 1 + count // 2 - 1, count - 1)
-        peer = lax.rem(me + ahead, count)
+        peer = flipped(me, count - step, count)
         return peer, pltpu.make_async_remote_copy(
             src_ref=outbox.at[step],
             dst_ref=out_ref.at[me],

time: 291 us -> 297 us (1.021)
  Pallas kernels: 88.8 us -> 94.1 us
    pallas_call x1, Pallas kernels: 78.3 us -> 83.6 us  [route(): pl.pallas_call(lambda *refs: route_kernel(count, *refs), name='route', ou...]
  transfers between devices with their start and end apart: 9 -> 9, of which waited for: 4 -> 4; matrix products, arithmetic and copies ran while one was open for 12% -> 11% of each run, Pallas kernels for 4% -> 4%
where the time goes in v5:
time: 297 us; the launch traced here: 296 us
  waiting for transfers between devices  104 us (35%)
  Pallas kernels  94.1 us (32%)
  starting transfers between devices  37.1 us (12%)
  matrix products  21.2 us (7%)
  local copies, waits for them, and re-layouts  17.1 us (6%)
  between operations  13.6 us (5%)
  other arithmetic  5.13 us (2%)
  blocking collectives  4.37 us (1%)
    pallas_call x1, Pallas kernels, route(): pl.pallas_call(lambda *refs: route_kernel(count, *refs), name='route', ou...  83.6 us
    all_gather x1, waiting for transfers between devices, shards(): lax.all_gather(w_qkv.reshape(w_qkv.shape[0], 3 * local_width), 'group', a...  40.4 us
    ppermute x3, waiting for transfers between devices, from_next(): lax.ppermute(value, axis, [((i + 1) % count, i) for i in range(count)])  34.6 us
    ppermute x3, starting transfers between devices, from_next(): lax.ppermute(value, axis, [((i + 1) % count, i) for i in range(count)])  34.2 us
    all_gather x1, waiting for transfers between devices, shards(): w_o = lax.all_gather(w_piece, 'group', axis=0, tiled=True)  28.6 us
    dot_general x1, matrix products, shards(): qkv = jnp.dot(normed, w_all, preferred_element_type=jnp.float32)  14.4 us
    pallas_call x1, Pallas kernels, attend(): pl.pallas_call(attend_kernel, grid=(width // HD,), out_shape=jax.ShapeDty...  10.5 us
    dot_general x2, matrix products, shards(): lax.dot_general(attended, lax.dynamic_index_in_dim(w_o, (me_tp + step) %...  6.78 us
  transfers between devices with their start and end apart: 9, of which 4 were waited for; matrix products, arithmetic and copies ran while one was open for 11% of the time, Pallas kernels for 4%

profile of v5, /device:TPU:1, one launch (start us, length us, event | category | flops | bytes accessed | tf_op | source)
XLA Modules:
  0.0 296.3 jit_solution(16648504252990482408)
XLA Ops:
  6.5 2.4 copy.27
  9.0 2.1 collective-permute-start
  11.1 0.2 broadcast_in_dim.10
  11.4 1.6 constant_dynamic-update-slice_fusion.1
  13.0 34.0 %collective-permute-done = bf16[512,1600]{0,1:T(8,128)(2,1)} collective-permute-done((bf16[512,1600]{0,1:T(8,128)(2,1)}, bf16[512,1600]{0,1:T(8,128)(2,1)}, u32[]{:S(2)}, u32[]{:S(2)}) %collective-permute-start) | collective-permute-done | bytes 1638432 | tf_op jit(solution)/shard_map/ppermute | solution.py:22
  47.0 1.6 constant_dynamic-update-slice_fusion
  48.6 1.4 collective-permute-start.5
  50.1 32.0 %collective-permute-start.1 = (bf16[1,1600]{1,0:T(2,128)(2,1)S(1)}, bf16[1,1600]{1,0:T(2,128)(2,1)S(1)}, u32[]{:S(2)}, u32[]{:S(2)}) collective-permute-start(bf16[1,1600]{1,0:T(2,128)(2,1)S(1)} %reshape.61), channel_id=1, source_target_pairs={{1,0},{0,1},{3,2},{2,3},{5,4},{4,5},{7,6},{6,7},{9,8},{8,9},{11,10... | collective-permute-start | bytes 9608 | tf_op jit(solution)/shard_map/ppermute | solution.py:22
  82.1 0.3 dynamic_update_slice.16
  82.4 0.7 collective-permute-done.1
  83.2 0.3 dynamic_update_slice.17
  83.4 0.8 fusion
  84.2 40.4 %all-gather.3.cloned.1.call-done = bf16[3200,3072]{1,0:T(8,128)(2,1)} async-done(((bf16[200,3072]{1,0:T(8,128)(2,1)}), bf16[3200,3072]{1,0:T(8,128)(2,1)}) %all-gather.3.cloned.1.call-update) | async-done | bytes 19660816 | tf_op jit(solution)/shard_map/all_gather | solution.py:170
  124.6 14.4 %fusion.3 = f32[512,3072]{1,0:T(8,128)S(1)} fusion(bf16[3200,3072]{1,0:T(8,128)(2,1)} %all-gather.3.cloned.1.call-done, bf16[512,3200]{0,1:T(8,128)(2,1)S(1)} %constant_dynamic-update-slice_fusion, f32[3200]{0:T(1024)S(1)} %mul.113, f32[512]{0:T(512)S(1)} %add_rsqrt_fusion.2), kind=kOutput, calls=%fused_computation.6 | convolution fusion | flops 10072883200 | bytes 29243904 | tf_op jit(solution)/shard_map/dot_general | solution.py:196
  139.1 2.5 copy-done.1
  141.6 0.3 multiply_reduce_fusion
  142.0 4.4 %all-reduce = (f32[512]{0:T(512)S(1)}, f32[512]{0:T(512)S(1)}) all-reduce(f32[512]{0:T(512)S(1)} %get-tuple-element.10, f32[512]{0:T(512)S(1)} %get-tuple-element.9), channel_id=1, replica_groups=mesh['group'=16,'tp'=2] {'tp'}, use_global_device_ids=true, to_apply=%region_5.6 | all-reduce | flops 1024 | bytes 8192 | tf_op jit(solution)/shard_map/psum | solution.py:200
  146.4 2.7 multiply_convert_fusion
  149.0 0.7 constant_dynamic-slice_fusion.1
  149.8 1.0 collective-permute-start.2
  150.8 0.7 constant_dynamic-slice_fusion
  151.6 0.5 collective-permute-start.4
  152.1 3.7 %copy.23 = f32[512,1600]{1,0:T(8,128)} copy(bf16[512,1600]{0,1:T(8,128)(2,1)} %param.8) | data formatting | bytes 4915200 | tf_op jit(solution)/shard_map/convert_element_type | solution.py:230
  155.9 10.5 %shard_map.82 = bf16[512,1024]{1,0:T(8,128)(2,1)} custom-call(bf16[512,1024]{1,0:T(8,128)(2,1)S(1)} %get-tuple-element.14.q_ref, bf16[512,1024]{1,0:T(8,128)(2,1)S(1)} %get-tuple-element.13.k_ref, bf16[512,1024]{1,0:T(8,128)(2,1)S(1)} %slice.39.v_ref, bf16[128,1024]{1,0:T(8,128)(2,1)} %collective-permute-done.2.kp_ref, ...), custom_call_target="tpu_custom_call" | custom-call | flops 1342177280 | bytes 4194304 | tf_op jit(solution)/shard_map/pallas_call | solution.py:50
  166.4 1.2 reduce-window.6
  167.6 0.2 slice_reduce_fusion
  168.0 28.6 %all-gather.5.cloned.1.call-done = bf16[3200,1024]{1,0:T(8,128)(2,1)} async-done(((bf16[200,1024]{1,0:T(8,128)(2,1)}), bf16[3200,1024]{1,0:T(8,128)(2,1)}) %all-gather.5.cloned.1.call-update) | async-done | bytes 6553616 | tf_op jit(solution)/shard_map/all_gather | solution.py:191
  196.6 4.5 %fusion.13 = bf16[512,1600]{1,0:T(8,128)(2,1)S(1)} fusion(bf16[512,1024]{1,0:T(8,128)(2,1)} %shard_map.82, bf16[2,1600,1024]{2,1,0:T(8,128)(2,1)} %bitcast.60, s32[]{:T(128)S(6)} %select_n.47), kind=kOutput, calls=%fused_computation.15 | convolution fusion | flops 1678540800 | bytes 5963780 | tf_op jit(solution)/shard_map/dot_general | solution.py:222
  201.1 0.7 copy-done.6
  201.8 2.3 add_convert_fusion.refs_1_
  204.1 83.6 %route.1 = bf16[16,64,1600]{2,1,0:T(8,128)(2,1)S(1)} custom-call(s32[1,512]{1,0:T(1,128)S(1)} %bitcast_add_fusion.refs_0_, bf16[512,1600]{1,0:T(8,128)(2,1)S(1)} %add_convert_fusion.refs_1_), custom_call_target="tpu_custom_call" | custom-call | flops 1677721600 | bytes 6553600 | tf_op jit(solution)/shard_map/route/pallas_call | solution.py:140
  287.7 1.8 copy.34
  (42 shorter events, 0.7 us)
Async XLA Ops:
  6.5 118.0 %all-gather.3.cloned.1.call-start = ((), (), s32[]{:S(2)}) async-start(), calls=%async_computation | async-start | bytes 20889600 | tf_op jit(solution)/shard_map/all_gather | solution.py:170
  9.0 187.6 %all-gather.5.cloned.1.call-start = ((), (), s32[]{:S(2)}) async-start(), calls=%async_computation.1 | async-start | bytes 6963200 | tf_op jit(solution)/shard_map/all_gather | solution.py:191
  9.0 38.0 %collective-permute-start = (bf16[512,1600]{0,1:T(8,128)(2,1)}, bf16[512,1600]{0,1:T(8,128)(2,1)}, u32[]{:S(2)}, u32[]{:S(2)}) collective-permute-start(bf16[512,1600]{0,1:T(8,128)(2,1)} %param.8), channel_id=1, source_target_pairs={{1,0},{0,1},{3,2},{2,3},{5,4},{4,5},{7,6},{6,7},{9,8},{8,9},{11,10... | collective-permute-start | bytes 4915208 | tf_op jit(solution)/shard_map/ppermute | solution.py:22
  11.3 37.2 %copy-start.7 = (bf16[1024,200]{0,1:T(8,128)(2,1)S(1)}, bf16[1024,200]{0,1:T(8,128)(2,1)}, u32[]{:S(2)}) copy-start(bf16[1024,200]{0,1:T(8,128)(2,1)} %param.12) | copy-start | bytes 1228804
  11.3 38.7 %copy-start.4 = (bf16[1600]{0:T(1024)(128)(2,1)S(1)}, bf16[1600]{0:T(1024)(128)(2,1)}, u32[]{:S(2)}) copy-start(bf16[1600]{0:T(1024)(128)(2,1)} %param.9) | copy-start | bytes 9604
  11.4 70.7 %copy-start.5 = (f32[2,1024]{1,0:T(2,128)S(1)}, f32[2,1024]{1,0:T(2,128)}, u32[]{:S(2)}) copy-start(f32[2,1024]{1,0:T(2,128)} %param.11) | copy-start | bytes 24580
  48.6 1.4 collective-permute-start.5
  50.1 33.1 %collective-permute-start.1 = (bf16[1,1600]{1,0:T(2,128)(2,1)S(1)}, bf16[1,1600]{1,0:T(2,128)(2,1)S(1)}, u32[]{:S(2)}, u32[]{:S(2)}) collective-permute-start(bf16[1,1600]{1,0:T(2,128)(2,1)S(1)} %reshape.61), channel_id=1, source_target_pairs={{1,0},{0,1},{3,2},{2,3},{5,4},{4,5},{7,6},{6,7},{9,8},{8,9},{11,10... | collective-permute-start | bytes 9608 | tf_op jit(solution)/shard_map/ppermute | solution.py:22
  139.0 2.7 copy-start.1
  146.3 5.1 %copy-start = (s32[512]{0:T(512)S(1)}, s32[512]{0:T(512)}, u32[]{:S(2)}) copy-start(s32[512]{0:T(512)} %param.14) | copy-start | bytes 6148
  149.8 6.1 %collective-permute-start.2 = (bf16[128,1024]{1,0:T(8,128)(2,1)}, bf16[128,1024]{1,0:T(8,128)(2,1)}, u32[]{:S(2)}, u32[]{:S(2)}) collective-permute-start(bf16[128,1024]{1,0:T(8,128)(2,1)} %constant_dynamic-slice_fusion.1), channel_id=1, source_target_pairs={{0,2},{2,0},{4,6},{6,4},{8,10},{10,8},{12,14},{14,12},{16,18},{18,... | collective-permute-start | bytes 786440 | tf_op jit(solution)/shard_map/ppermute | solution.py:17
  151.5 4.4 %collective-permute-start.3 = (bf16[128,1024]{1,0:T(8,128)(2,1)}, bf16[128,1024]{1,0:T(8,128)(2,1)}, u32[]{:S(2)}, u32[]{:S(2)}) collective-permute-start(bf16[128,1024]{1,0:T(8,128)(2,1)} %constant_dynamic-slice_fusion), channel_id=1, source_target_pairs={{0,2},{2,0},{4,6},{6,4},{8,10},{10,8},{12,14},{14,12},{16,18},{18,... | collective-permute-start | bytes 786440 | tf_op jit(solution)/shard_map/ppermute | solution.py:17
  151.6 4.3 %collective-permute-start.4 = (s32[128]{0:T(128)S(1)}, s32[128]{0:T(128)S(1)}, u32[]{:S(2)}, u32[]{:S(2)}) collective-permute-start(s32[128]{0:T(128)S(1)} %dynamic_slice.18), channel_id=1, source_target_pairs={{0,2},{2,0},{4,6},{6,4},{8,10},{10,8},{12,14},{14,12},{16,18},{18,... | collective-permute-start | bytes 1544 | tf_op jit(solution)/shard_map/ppermute | solution.py:17
  155.7 10.7 %copy-start.3 = (s32[512,1]{0,1:T(1,128)S(1)}, s32[512,1]{0,1:T(1,128)}, u32[]{:S(2)}) copy-start(s32[512,1]{0,1:T(1,128)} %param.15) | copy-start | bytes 6148
  166.4 34.7 %collective-permute-start.6 = (bf16[512,1024]{1,0:T(8,128)(2,1)}, bf16[512,1024]{1,0:T(8,128)(2,1)S(1)}, u32[]{:S(2)}, u32[]{:S(2)}) collective-permute-start(bf16[512,1024]{1,0:T(8,128)(2,1)} %shard_map.82), channel_id=1, source_target_pairs={{1,0},{0,1},{3,2},{2,3},{5,4},{4,5},{7,6},{6,7},{9,8},{8,9},{11,10... | collective-permute-start | bytes 3145736 | tf_op jit(solution)/shard_map/ppermute | solution.py:22
  196.6 4.5 %copy-start.2 = (f32[512,1600]{1,0:T(8,128)S(1)}, f32[512,1600]{1,0:T(8,128)}, u32[]{:S(2)}) copy-start(f32[512,1600]{1,0:T(8,128)} %copy.23) | copy-start | bytes 9830404
  196.6 5.2 %copy-start.6 = (bf16[3200,1024]{1,0:T(8,128)(2,1)S(1)}, bf16[3200,1024]{1,0:T(8,128)(2,1)}, u32[]{:S(2)}) copy-start(bf16[3200,1024]{1,0:T(8,128)(2,1)} %all-gather.5.cloned.1.call-done) | copy-start | bytes 19660804
  196.6 5.2 %copy-start.8 = (f32[1600]{0:T(1024)S(1)}, f32[1600]{0:T(1024)}, u32[]{:S(2)}) copy-start(f32[1600]{0:T(1024)} %param.13) | copy-start | bytes 19204
Sparse Core Ops, SparseCore 0:
  9.1 115.4 all-gather.2
  126.9 69.6 all-gather.4
